TPU v7x, 32 devices: a whole 2x2x4 slice. The times are simulated.
32 devices in a mesh: dp: 8 (over y, x, core), fsdp: 4 (over z).
Axes of the slice: x: 2, y: 2, z: 4, core: 2. Of those that a mesh axis runs over, the one named last changes fastest.
Arguments:
- state: bfloat16 [3, 8192, 512], P(None, ('dp', 'fsdp')), may hold values from -6 to 6
- segment: int32 [3, 8192], P(None, 'dp'), may hold values from 0 to 12, as said below
- parent: int32 [3, 8, 13], P(None, 'dp'), may hold values from 0 to 11, as said below
- halting: float32 [3, 8192], P(None, ('dp', 'fsdp')), may hold values from 0 to 1
- ponder: float32 [3, 8192], P(None, ('dp', 'fsdp')), may hold values from 1 to 4
- cot_state: bfloat16 [3, 8192, 512], P(None, ('dp', 'fsdp')), may hold values from -6 to 6
- cot_halt: float32 [3, 8192], P(None, ('dp', 'fsdp')), may hold values from -12 to 12
- w_query: bfloat16 [512, 512], P(('dp', 'fsdp')), may hold values from -0.25 to 0.25
- w_key: bfloat16 [512, 512], P(('dp', 'fsdp')), may hold values from -0.25 to 0.25
- w_value: bfloat16 [512, 512], P(('dp', 'fsdp')), may hold values from -0.25 to 0.25
- w_out: bfloat16 [512, 512], P(('dp', 'fsdp')), may hold values from -1 to 1
- w_up: bfloat16 [512, 2048], P(('dp', 'fsdp')), may hold values from -0.25 to 0.25
- b_up: bfloat16 [2048], P(('dp', 'fsdp')), may hold values from -3 to 3
- w_down: bfloat16 [2048, 512], P(('dp', 'fsdp')), may hold values from -0.125 to 0.125
- b_down: bfloat16 [512], P(('dp', 'fsdp')), may hold values from -3 to 3
- gain_one: bfloat16 [512], P(('dp', 'fsdp')), may hold values from 0.5 to 1.5
- bias_one: bfloat16 [512], P(('dp', 'fsdp')), may hold values from -3 to 3
- gain_two: bfloat16 [512], P(('dp', 'fsdp')), may hold values from 0.5 to 1.5
- bias_two: bfloat16 [512], P(('dp', 'fsdp')), may hold values from -3 to 3
- w_halt: bfloat16 [512], P(('dp', 'fsdp')), may hold values from -0.25 to 0.25
Outputs:
- new_state: bfloat16 [3, 8192, 512], P(None, ('dp', 'fsdp'))
- new_halting: float32 [3, 8192], P(None, ('dp', 'fsdp'))
- new_ponder: float32 [3, 8192], P(None, ('dp', 'fsdp'))
- grad_state: float32 [3, 8192, 512], P(None, ('dp', 'fsdp'))
- grad_w_query: float32 [512, 512], P(('dp', 'fsdp'))
- grad_w_key: float32 [512, 512], P(('dp', 'fsdp'))
- grad_w_value: float32 [512, 512], P(('dp', 'fsdp'))
- grad_w_out: float32 [512, 512], P(('dp', 'fsdp'))
- grad_w_up: float32 [512, 2048], P(('dp', 'fsdp'))
- grad_b_up: float32 [2048], P(('dp', 'fsdp'))
- grad_w_down: float32 [2048, 512], P(('dp', 'fsdp'))
- grad_b_down: float32 [512], P(('dp', 'fsdp'))
- grad_gain_one: float32 [512], P(('dp', 'fsdp'))
- grad_bias_one: float32 [512], P(('dp', 'fsdp'))
- grad_gain_two: float32 [512], P(('dp', 'fsdp'))
- grad_bias_two: float32 [512], P(('dp', 'fsdp'))
- grad_w_halt: float32 [512], P(('dp', 'fsdp'))
Inputs may be any that keep to these rules, and one draw needn't show every extreme that they name: Within each tree of 1024 tokens the segment ids never fall, the first token has segment 0, the last has 12, and segment 0 covers at least the first 256 tokens. parent[m, t, 0] is 0 and parent[m, t, k] lies in 0 to k - 1: segment k of tree t hangs under segment parent[m, t, k].
All inputs are finite; a program needn't handle non-finite values.
Results may differ from a plain program's by a relative error of at most 0.018.
Values may be sent and summed in bfloat16 or wider, within the bound.
A program may use at most 128 MiB of HBM per device.

v0:
```python
import math

import jax
import jax.numpy as jnp
from jax import lax
from jax.sharding import PartitionSpec as P

HEADS = 8


EPS = 1e-06
NEG = -1000000000.0
HALT_LIMIT = 0.99
GELU_C = math.sqrt(2.0 / math.pi)
GELU_A = 0.044715


def gelu_parts(values):
    inner = GELU_C * (values + GELU_A * values * values * values)
    tanh_val = jnp.tanh(inner)
    result = 0.5 * values * (1.0 + tanh_val)
    slope = 0.5 * (1.0 + tanh_val) + 0.5 * values * (1.0 - tanh_val * tanh_val) * GELU_C * (
        1.0 + 3.0 * GELU_A * values * values
    )
    return (result, slope)


def timing(positions, model_width):
    half_width = model_width // 2
    freq_rates = jnp.exp(
        -math.log(10000.0) * jnp.arange(half_width, dtype=jnp.float32) / half_width
    )
    angles = positions[:, None] * freq_rates[None, :]
    return jnp.concatenate([jnp.sin(angles), jnp.cos(angles)], axis=1)


def reach_table(parent_row):
    seg_count = parent_row.shape[0]
    labels = jnp.arange(seg_count, dtype=jnp.int32)
    parent_hot = (parent_row[:, None] == labels[None, :]).astype(jnp.int32)
    walker = (labels[:, None] == labels[None, :]).astype(jnp.int32)
    reach_all = walker
    for repeat in range(seg_count):
        walker = jnp.dot(walker, parent_hot)
        reach_all = jnp.maximum(reach_all, walker)
    return reach_all


def allowed_mask(query_seg, key_seg, reach_all):
    seg_count = reach_all.shape[0]
    labels = jnp.arange(seg_count, dtype=jnp.int32)
    query_hot = (query_seg[:, None] == labels[None, :]).astype(jnp.bfloat16)
    key_hot = (key_seg[:, None] == labels[None, :]).astype(jnp.bfloat16)
    path_hits = jnp.dot(
        query_hot, reach_all.astype(jnp.bfloat16), preferred_element_type=jnp.float32
    ).astype(jnp.bfloat16)
    return (
        lax.dot_general(
            path_hits, key_hot, (((1,), (1,)), ((), ())), preferred_element_type=jnp.float32
        )
        > 0.5
    )


def contract_rows(first_mat, second_mat):
    return lax.dot_general(
        first_mat, second_mat, (((0,), (0,)), ((), ())), preferred_element_type=jnp.float32
    )


def contract_cols(first_mat, second_mat):
    return lax.dot_general(
        first_mat, second_mat, (((1,), (1,)), ((), ())), preferred_element_type=jnp.float32
    )


def layer_norm(values):
    centered = values - jnp.mean(values, axis=-1, keepdims=True)
    variance = jnp.mean(centered * centered, axis=-1, keepdims=True)
    inv_std = lax.rsqrt(variance + EPS)
    return (centered * inv_std, inv_std)


def norm_back(grad_norm, normal, inv_std):
    grad_mean = jnp.mean(grad_norm, axis=-1, keepdims=True)
    cross_mean = jnp.mean(grad_norm * normal, axis=-1, keepdims=True)
    return inv_std * (grad_norm - grad_mean - normal * cross_mean)


def attention_forward(queries, keys_all, values_all, allowed):
    row_count, model_width = queries.shape
    head_size = model_width // HEADS
    pair_width = 2 * head_size
    score_scale = head_size ** (-0.5)
    tree_len = keys_all.shape[0]

    def one_pair(index, carry):
        mixed_out, log_sums = carry
        column = index * pair_width
        query_pair = lax.dynamic_slice_in_dim(queries, column, pair_width, 1).reshape(
            row_count, 2, head_size
        )
        key_pair = lax.dynamic_slice_in_dim(keys_all, column, pair_width, 1).reshape(
            tree_len, 2, head_size
        )
        value_pair = lax.dynamic_slice_in_dim(values_all, column, pair_width, 1).reshape(
            tree_len, 2, head_size
        )
        scores = (
            jnp.einsum("rhd,khd->hrk", query_pair, key_pair, preferred_element_type=jnp.float32)
            * score_scale
        )
        scores = jnp.where(allowed[None], scores, NEG)
        largest = jnp.max(scores, axis=-1, keepdims=True)
        exp_scores = jnp.exp(scores - largest)
        row_totals = jnp.sum(exp_scores, axis=-1, keepdims=True)
        softmax_out = (exp_scores / row_totals).astype(jnp.bfloat16)
        pair_out = jnp.einsum(
            "hrk,khd->rhd", softmax_out, value_pair, preferred_element_type=jnp.float32
        )
        mixed_out = lax.dynamic_update_slice_in_dim(
            mixed_out, pair_out.reshape(row_count, pair_width), column, 1
        )
        log_sums = lax.dynamic_update_slice_in_dim(
            log_sums, (largest + jnp.log(row_totals))[None], index, 0
        )
        return (mixed_out, log_sums)

    initial = (
        jnp.zeros((row_count, model_width), jnp.float32),
        jnp.zeros((HEADS // 2, 2, row_count, 1), jnp.float32),
    )
    return lax.fori_loop(0, HEADS // 2, one_pair, initial)


def attention_backward(queries, keys_all, values_all, allowed, log_sums, grad_mixed):
    row_count, model_width = queries.shape
    head_size = model_width // HEADS
    pair_width = 2 * head_size
    score_scale = head_size ** (-0.5)
    tree_len = keys_all.shape[0]

    def one_pair(index, carry):
        grad_query, grad_keys, grad_values = carry
        column = index * pair_width
        query_pair = lax.dynamic_slice_in_dim(queries, column, pair_width, 1).reshape(
            row_count, 2, head_size
        )
        key_pair = lax.dynamic_slice_in_dim(keys_all, column, pair_width, 1).reshape(
            tree_len, 2, head_size
        )
        value_pair = lax.dynamic_slice_in_dim(values_all, column, pair_width, 1).reshape(
            tree_len, 2, head_size
        )
        grad_pair = lax.dynamic_slice_in_dim(grad_mixed, column, pair_width, 1).reshape(
            row_count, 2, head_size
        )
        scores = (
            jnp.einsum("rhd,khd->hrk", query_pair, key_pair, preferred_element_type=jnp.float32)
            * score_scale
        )
        scores = jnp.where(allowed[None], scores, NEG)
        pair_sums = lax.dynamic_index_in_dim(log_sums, index, 0, keepdims=False)
        softmax_full = jnp.exp(scores - pair_sums)
        grad_soft = jnp.einsum(
            "rhd,khd->hrk", grad_pair, value_pair, preferred_element_type=jnp.float32
        )
        inner_sum = jnp.sum(grad_soft * softmax_full, axis=-1, keepdims=True)
        grad_scores = (softmax_full * (grad_soft - inner_sum) * score_scale).astype(jnp.bfloat16)
        query_part = jnp.einsum(
            "hrk,khd->rhd", grad_scores, key_pair, preferred_element_type=jnp.float32
        )
        key_part = jnp.einsum(
            "hrk,rhd->khd", grad_scores, query_pair, preferred_element_type=jnp.float32
        )
        value_part = jnp.einsum(
            "hrk,rhd->khd",
            softmax_full.astype(jnp.bfloat16),
            grad_pair,
            preferred_element_type=jnp.float32,
        )
        grad_query = lax.dynamic_update_slice_in_dim(
            grad_query, query_part.reshape(row_count, pair_width), column, 1
        )
        grad_keys = lax.dynamic_update_slice_in_dim(
            grad_keys, key_part.reshape(tree_len, pair_width), column, 1
        )
        grad_values = lax.dynamic_update_slice_in_dim(
            grad_values, value_part.reshape(tree_len, pair_width), column, 1
        )
        return (grad_query, grad_keys, grad_values)

    initial = (
        jnp.zeros((row_count, model_width), jnp.float32),
        jnp.zeros((tree_len, model_width), jnp.float32),
        jnp.zeros((tree_len, model_width), jnp.float32),
    )
    return lax.fori_loop(0, HEADS // 2, one_pair, initial)


def per_device(
    state,
    segment,
    parent,
    halting,
    ponder,
    cot_state,
    cot_halt,
    w_query,
    w_key,
    w_value,
    w_out,
    w_up,
    b_up,
    w_down,
    b_down,
    gain_one,
    bias_one,
    gain_two,
    bias_two,
    w_halt,
):
    micro_count, row_count, model_width = state.shape
    fsdp_index = lax.axis_index("fsdp")
    devices = lax.axis_size("dp") * lax.axis_size("fsdp")
    positions = (fsdp_index * row_count + jnp.arange(row_count, dtype=jnp.int32)).astype(
        jnp.float32
    )
    signal = timing(positions, model_width)
    accum = [
        jnp.zeros((shard.shape[0] * devices,) + shard.shape[1:], jnp.float32)
        for shard in (
            w_query,
            w_key,
            w_value,
            w_out,
            w_up,
            b_up,
            w_down,
            b_down,
            gain_one,
            bias_one,
            gain_two,
            bias_two,
            w_halt,
        )
    ]
    state_list = []
    halt_list = []
    ponder_list = []
    grad_list = []
    for micro in range(micro_count):
        (
            query_mat,
            key_mat,
            value_mat,
            out_mat,
            up_mat,
            up_bias,
            down_mat,
            down_bias,
            gain_a,
            bias_a,
            gain_b,
            bias_b,
            halt_weights,
        ) = (
            lax.all_gather(w_query, ("dp", "fsdp"), axis=0, tiled=True),
            lax.all_gather(w_key, ("dp", "fsdp"), axis=0, tiled=True),
            lax.all_gather(w_value, ("dp", "fsdp"), axis=0, tiled=True),
            lax.all_gather(w_out, ("dp", "fsdp"), axis=0, tiled=True),
            lax.all_gather(w_up, ("dp", "fsdp"), axis=0, tiled=True),
            lax.all_gather(b_up, ("dp", "fsdp"), axis=0, tiled=True),
            lax.all_gather(w_down, ("dp", "fsdp"), axis=0, tiled=True),
            lax.all_gather(b_down, ("dp", "fsdp"), axis=0, tiled=True),
            lax.all_gather(gain_one, ("dp", "fsdp"), axis=0, tiled=True),
            lax.all_gather(bias_one, ("dp", "fsdp"), axis=0, tiled=True),
            lax.all_gather(gain_two, ("dp", "fsdp"), axis=0, tiled=True),
            lax.all_gather(bias_two, ("dp", "fsdp"), axis=0, tiled=True),
            lax.all_gather(w_halt, ("dp", "fsdp"), axis=0, tiled=True),
        )
        state_in = state[micro].astype(jnp.float32)
        signal_in = state_in + signal
        normed = signal_in.astype(jnp.bfloat16)
        queries = jnp.dot(normed, query_mat, preferred_element_type=jnp.float32).astype(
            jnp.bfloat16
        )
        keys_own = jnp.dot(normed, key_mat, preferred_element_type=jnp.float32).astype(jnp.bfloat16)
        values_own = jnp.dot(normed, value_mat, preferred_element_type=jnp.float32).astype(
            jnp.bfloat16
        )
        keys_all, values_all = (
            lax.all_gather(keys_own, "fsdp", axis=0, tiled=True),
            lax.all_gather(values_own, "fsdp", axis=0, tiled=True),
        )
        seg_tree = segment[micro]
        seg_rows = lax.dynamic_slice_in_dim(seg_tree, fsdp_index * row_count, row_count)
        allowed = allowed_mask(seg_rows, seg_tree, reach_table(parent[micro, 0]))
        mixed, log_sums = attention_forward(queries, keys_all, values_all, allowed)
        mixed_b = mixed.astype(jnp.bfloat16)
        attended = jnp.dot(mixed_b, out_mat, preferred_element_type=jnp.float32)
        norm_one, inv_one = layer_norm(signal_in + attended)
        gain_a32 = gain_a.astype(jnp.float32)
        gain_b32 = gain_b.astype(jnp.float32)
        first_out = norm_one * gain_a32 + bias_a.astype(jnp.float32)
        first_b = first_out.astype(jnp.bfloat16)
        pre_act = jnp.dot(first_b, up_mat, preferred_element_type=jnp.float32) + up_bias.astype(
            jnp.float32
        )
        activated, act_slope = gelu_parts(pre_act)
        hidden = activated.astype(jnp.bfloat16)
        down_out = jnp.dot(hidden, down_mat, preferred_element_type=jnp.float32) + down_bias.astype(
            jnp.float32
        )
        norm_two, inv_two = layer_norm(first_out + down_out)
        second_out = norm_two * gain_b32 + bias_b.astype(jnp.float32)
        halt_vec = halt_weights.astype(jnp.float32)
        halt_prob = jax.nn.sigmoid(jnp.sum(second_out * halt_vec, axis=1))
        halting_row = halting[micro]
        running = (halting_row < HALT_LIMIT).astype(jnp.float32)
        weight = running * halt_prob * (1.0 - halting_row)
        mixed_state = weight[:, None] * second_out + (1.0 - weight[:, None]) * state_in
        state_list.append(mixed_state.astype(jnp.bfloat16))
        halt_list.append(halting_row + weight)
        ponder_list.append(ponder[micro] + running * (1.0 - weight))
        (
            query_mat,
            key_mat,
            value_mat,
            out_mat,
            up_mat,
            up_bias,
            down_mat,
            down_bias,
            gain_a,
            bias_a,
            gain_b,
            bias_b,
            halt_weights,
        ) = (
            lax.all_gather(w_query, ("dp", "fsdp"), axis=0, tiled=True),
            lax.all_gather(w_key, ("dp", "fsdp"), axis=0, tiled=True),
            lax.all_gather(w_value, ("dp", "fsdp"), axis=0, tiled=True),
            lax.all_gather(w_out, ("dp", "fsdp"), axis=0, tiled=True),
            lax.all_gather(w_up, ("dp", "fsdp"), axis=0, tiled=True),
            lax.all_gather(b_up, ("dp", "fsdp"), axis=0, tiled=True),
            lax.all_gather(w_down, ("dp", "fsdp"), axis=0, tiled=True),
            lax.all_gather(b_down, ("dp", "fsdp"), axis=0, tiled=True),
            lax.all_gather(gain_one, ("dp", "fsdp"), axis=0, tiled=True),
            lax.all_gather(bias_one, ("dp", "fsdp"), axis=0, tiled=True),
            lax.all_gather(gain_two, ("dp", "fsdp"), axis=0, tiled=True),
            lax.all_gather(bias_two, ("dp", "fsdp"), axis=0, tiled=True),
            lax.all_gather(w_halt, ("dp", "fsdp"), axis=0, tiled=True),
        )
        grad_new = cot_state[micro].astype(jnp.float32)
        grad_weight = jnp.sum(grad_new * (second_out - state_in), axis=1) + cot_halt[micro]
        grad_logit = grad_weight * running * (1.0 - halting_row) * halt_prob * (1.0 - halt_prob)
        grad_second = weight[:, None] * grad_new + grad_logit[:, None] * halt_vec
        grad_halt_vec = jnp.sum(grad_logit[:, None] * second_out, axis=0)
        grad_gain_b = jnp.sum(grad_second * norm_two, axis=0)
        grad_bias_b = jnp.sum(grad_second, axis=0)
        grad_sum_two = norm_back(grad_second * gain_b32, norm_two, inv_two)
        grad_down_b = grad_sum_two.astype(jnp.bfloat16)
        grad_down_bias = jnp.sum(grad_sum_two, axis=0)
        grad_down_mat = contract_rows(hidden, grad_down_b)
        grad_hidden = contract_cols(grad_down_b, down_mat)
        grad_pre = grad_hidden * act_slope
        grad_up_bias = jnp.sum(grad_pre, axis=0)
        grad_pre_b = grad_pre.astype(jnp.bfloat16)
        grad_up_mat = contract_rows(first_b, grad_pre_b)
        grad_first = grad_sum_two + contract_cols(grad_pre_b, up_mat)
        grad_gain_a = jnp.sum(grad_first * norm_one, axis=0)
        grad_bias_a = jnp.sum(grad_first, axis=0)
        grad_sum_one = norm_back(grad_first * gain_a32, norm_one, inv_one)
        grad_att_b = grad_sum_one.astype(jnp.bfloat16)
        grad_out_mat = contract_rows(mixed_b, grad_att_b)
        grad_mixed = contract_cols(grad_att_b, out_mat).astype(jnp.bfloat16)
        grad_query, grad_keys_all, grad_values_all = attention_backward(
            queries, keys_all, values_all, allowed, log_sums, grad_mixed
        )
        grad_keys, grad_values = (
            lax.psum_scatter(
                grad_keys_all.astype(jnp.bfloat16), "fsdp", scatter_dimension=0, tiled=True
            ).astype(jnp.float32),
            lax.psum_scatter(
                grad_values_all.astype(jnp.bfloat16), "fsdp", scatter_dimension=0, tiled=True
            ).astype(jnp.float32),
        )
        grad_query_b = grad_query.astype(jnp.bfloat16)
        grad_keys_b = grad_keys.astype(jnp.bfloat16)
        grad_values_b = grad_values.astype(jnp.bfloat16)
        grad_query_mat = contract_rows(normed, grad_query_b)
        grad_key_mat = contract_rows(normed, grad_keys_b)
        grad_value_mat = contract_rows(normed, grad_values_b)
        grad_normed = (
            contract_cols(grad_query_b, query_mat)
            + contract_cols(grad_keys_b, key_mat)
            + contract_cols(grad_values_b, value_mat)
        )
        grad_list.append(grad_sum_one + grad_normed + (1.0 - weight[:, None]) * grad_new)
        terms = (
            grad_query_mat,
            grad_key_mat,
            grad_value_mat,
            grad_out_mat,
            grad_up_mat,
            grad_up_bias,
            grad_down_mat,
            grad_down_bias,
            grad_gain_a,
            grad_bias_a,
            grad_gain_b,
            grad_bias_b,
            grad_halt_vec,
        )
        accum = [total + term for total, term in zip(accum, terms)]
    summed = (
        lax.psum_scatter(accum[0], ("dp", "fsdp"), scatter_dimension=0, tiled=True),
        lax.psum_scatter(accum[1], ("dp", "fsdp"), scatter_dimension=0, tiled=True),
        lax.psum_scatter(accum[2], ("dp", "fsdp"), scatter_dimension=0, tiled=True),
        lax.psum_scatter(accum[3], ("dp", "fsdp"), scatter_dimension=0, tiled=True),
        lax.psum_scatter(accum[4], ("dp", "fsdp"), scatter_dimension=0, tiled=True),
        lax.psum_scatter(accum[5], ("dp", "fsdp"), scatter_dimension=0, tiled=True),
        lax.psum_scatter(accum[6], ("dp", "fsdp"), scatter_dimension=0, tiled=True),
        lax.psum_scatter(accum[7], ("dp", "fsdp"), scatter_dimension=0, tiled=True),
        lax.psum_scatter(accum[8], ("dp", "fsdp"), scatter_dimension=0, tiled=True),
        lax.psum_scatter(accum[9], ("dp", "fsdp"), scatter_dimension=0, tiled=True),
        lax.psum_scatter(accum[10], ("dp", "fsdp"), scatter_dimension=0, tiled=True),
        lax.psum_scatter(accum[11], ("dp", "fsdp"), scatter_dimension=0, tiled=True),
        lax.psum_scatter(accum[12], ("dp", "fsdp"), scatter_dimension=0, tiled=True),
    )
    return (
        jnp.stack(state_list),
        jnp.stack(halt_list),
        jnp.stack(ponder_list),
        jnp.stack(grad_list),
        summed[0],
        summed[1],
        summed[2],
        summed[3],
        summed[4],
        summed[5],
        summed[6],
        summed[7],
        summed[8],
        summed[9],
        summed[10],
        summed[11],
        summed[12],
    )


def solution(mesh):
    placed = (
        P(None, ("dp", "fsdp"), None),
        P(None, "dp"),
        P(None, "dp", None),
        P(None, ("dp", "fsdp")),
        P(None, ("dp", "fsdp")),
        P(None, ("dp", "fsdp"), None),
        P(None, ("dp", "fsdp")),
        P(("dp", "fsdp"), None),
        P(("dp", "fsdp"), None),
        P(("dp", "fsdp"), None),
        P(("dp", "fsdp"), None),
        P(("dp", "fsdp"), None),
        P(("dp", "fsdp")),
        P(("dp", "fsdp"), None),
        P(("dp", "fsdp")),
        P(("dp", "fsdp")),
        P(("dp", "fsdp")),
        P(("dp", "fsdp")),
        P(("dp", "fsdp")),
        P(("dp", "fsdp")),
    )
    return jax.shard_map(
        per_device,
        mesh=mesh,
        in_specs=placed,
        out_specs=(
            P(None, ("dp", "fsdp"), None),
            P(None, ("dp", "fsdp")),
            P(None, ("dp", "fsdp")),
            P(None, ("dp", "fsdp"), None),
            P(("dp", "fsdp"), None),
            P(("dp", "fsdp"), None),
            P(("dp", "fsdp"), None),
            P(("dp", "fsdp"), None),
            P(("dp", "fsdp"), None),
            P(("dp", "fsdp")),
            P(("dp", "fsdp"), None),
            P(("dp", "fsdp")),
            P(("dp", "fsdp")),
            P(("dp", "fsdp")),
            P(("dp", "fsdp")),
            P(("dp", "fsdp")),
            P(("dp", "fsdp")),
        ),
        check_vma=False,
    )
```

profile of v0, /device:TPU:0, one launch (start us, length us, event | category | flops | bytes accessed | tf_op | source)
XLA Modules:
  0.0 1624.2 jit_solution(14131632104009593285)
XLA Ops:
  7.3 74.2 %all_gather.38 = bf16[512,512]{1,0:T(8,128)(2,1)S(1)} all-gather(bf16[16,512]{1,0:T(8,128)(2,1)} %param.41), channel_id=1, replica_groups=mesh['dp'=8,'fsdp'=4] {'dp','fsdp'}, dimensions={0}, use_global_device_ids=true | all-gather | bytes 540672 | tf_op jit(solution)/shard_map/all_gather | solution.py:270
  85.1 70.3 %all_gather.41 = bf16[512,512]{1,0:T(8,128)(2,1)S(1)} all-gather(bf16[16,512]{1,0:T(8,128)(2,1)S(1)} %copy-done.108), channel_id=1, replica_groups=mesh['dp'=8,'fsdp'=4] {'dp','fsdp'}, dimensions={0}, use_global_device_ids=true | all-gather | bytes 540672 | tf_op jit(solution)/shard_map/all_gather | solution.py:269
  163.0 75.7 %all_gather.40 = bf16[512,512]{1,0:T(8,128)(2,1)S(1)} all-gather(bf16[16,512]{1,0:T(8,128)(2,1)S(1)} %copy-done.109), channel_id=1, replica_groups=mesh['dp'=8,'fsdp'=4] {'dp','fsdp'}, dimensions={0}, use_global_device_ids=true | all-gather | bytes 540672 | tf_op jit(solution)/shard_map/all_gather | solution.py:268
  241.5 38.7 %all-reduce.15 = (bf16[512]{0:T(512)(128)(2,1)S(1)}, bf16[512]{0:T(512)(128)(2,1)S(1)}, bf16[512]{0:T(512)(128)(2,1)S(1)}, bf16[512]{0:T(512)(128)(2,1)S(1)}, bf...) all-reduce(bf16[512]{0:T(512)(128)(2,1)S(1)} %dynamic-update-slice., ...), channel_id=1, replica_groups=mesh['dp'=8,'fsdp'=4] {'dp','fsdp'}, use_global_device_ids=true, to_apply=%add.5 | all-reduce | flops 5120 | bytes 20480
  284.3 73.5 %all_gather.43 = bf16[512,512]{1,0:T(8,128)(2,1)S(1)} all-gather(bf16[16,512]{1,0:T(8,128)(2,1)S(1)} %copy-done.110), channel_id=1, replica_groups=mesh['dp'=8,'fsdp'=4] {'dp','fsdp'}, dimensions={0}, use_global_device_ids=true | all-gather | bytes 540672 | tf_op jit(solution)/shard_map/all_gather | solution.py:271
  370.7 15.9 while.96
  392.1 18.1 %while.97 = (s32[]{:T(128)}, bf16[256,512]{0,1:T(8,128)(2,1)S(1)}, f32[4,2,256,1]{2,1,3,0:T(2,128)}, bf16[1024,512]{0,1:T(8,128)(2,1)S(1)}, pred[256,1024]{1,0:T...) while((s32[]{:T(128)}, bf16[256,512]{0,1:T(8,128)(2,1)S(1)}, ...), condition=%wide.region_12.13_spmd, body=%wide.region_9.12_spmd.sunk | while | flops 140508672 | bytes 9060531 | solution.py:133
  415.8 18.5 %while.98 = (s32[]{:T(128)}, bf16[256,512]{0,1:T(8,128)(2,1)}, f32[4,2,256,1]{2,1,3,0:T(2,128)S(1)}, bf16[1024,512]{0,1:T(8,128)(2,1)S(1)}, pred[256,1024]{1,0:T...) while((s32[]{:T(128)}, bf16[256,512]{0,1:T(8,128)(2,1)}, ...), condition=%wide.region_21.22_spmd, body=%wide.region_18.21_spmd.sunk | while | flops 140508672 | bytes 9060531 | solution.py:133
  439.6 3.7 convolution_add_fusion.2
  443.3 3.3 fusion.303
  478.1 55.1 %while.99 = (s32[]{:T(128)}, bf16[256,512]{0,1:T(8,128)(2,1)}, bf16[1024,512]{0,1:T(8,128)(2,1)}, bf16[1024,512]{0,1:T(8,128)(2,1)}, bf16[1024,512]{0,1:T(8,128)...) while((s32[]{:T(128)}, bf16[256,512]{0,1:T(8,128)(2,1)}, ...), condition=%wide.region_34.35_spmd, body=%wide.region_32.34_spmd.sunk | while | flops 342887424 | bytes 19208408 | solution.py:198
  484.4 2.9 fusion.562
  488.2 2.8 fusion.564
  498.2 2.9 fusion.562
  502.0 2.8 fusion.564
  512.0 2.9 fusion.562
  515.8 2.8 fusion.564
  525.7 2.9 fusion.562
  529.5 2.8 fusion.564
  536.2 70.6 %while.100 = (s32[]{:T(128)}, bf16[256,512]{0,1:T(8,128)(2,1)}, bf16[1024,512]{0,1:T(8,128)(2,1)}, bf16[1024,512]{0,1:T(8,128)(2,1)}, bf16[1024,512]{0,1:T(8,128...) while((s32[]{:T(128)}, bf16[256,512]{0,1:T(8,128)(2,1)}, ...), condition=%wide.region_44.45_spmd, body=%wide.region_42.44_spmd.sunk | while | flops 342887424 | bytes 19732752 | solution.py:198
  543.3 3.6 fusion.576
  548.6 3.5 fusion.578
  560.9 3.5 fusion.576
  566.3 3.5 fusion.578
  578.6 3.5 fusion.576
  583.9 3.5 fusion.578
  596.2 3.5 fusion.576
  601.5 3.5 fusion.578
  612.9 55.8 %while.101 = (s32[]{:T(128)}, bf16[256,512]{0,1:T(8,128)(2,1)S(1)}, bf16[1024,512]{0,1:T(8,128)(2,1)}, bf16[1024,512]{0,1:T(8,128)(2,1)}, bf16[1024,512]{0,1:T(8...) while((s32[]{:T(128)}, bf16[256,512]{0,1:T(8,128)(2,1)S(1)}, ...), condition=%wide.region_54.55_spmd, body=%wide.region_52.54_spmd.sunk | while | flops 342887424 | bytes 19208408 | solution.py:198
  620.3 2.9 fusion.590
  623.5 2.8 fusion.592
  634.2 2.9 fusion.590
  637.4 2.8 fusion.592
  648.1 2.9 fusion.590
  661.9 2.9 fusion.590
  681.9 12.0 reduce-scatter.21.cloned.1.call-done
  696.3 25.6 %reduce-scatter.15.cloned.1.call-done = bf16[256,512]{0,1:T(8,128)(2,1)} async-done(((bf16[1024,512]{0,1:T(8,128)(2,1)}), bf16[256,512]{0,1:T(8,128)(2,1)}) %reduce-scatter.15.cloned.1.call-update) | async-done | bytes 262160 | tf_op jit(solution)/shard_map/reduce_scatter | solution.py:385
  724.2 25.9 %reduce-scatter.19.cloned.1.call-done = bf16[256,512]{0,1:T(8,128)(2,1)} async-done(((bf16[1024,512]{0,1:T(8,128)(2,1)}), bf16[256,512]{0,1:T(8,128)(2,1)}) %reduce-scatter.19.cloned.1.call-update) | async-done | bytes 262160 | tf_op jit(solution)/shard_map/reduce_scatter | solution.py:385
  751.8 26.4 %reduce-scatter.23.cloned.1.call-done = bf16[256,512]{0,1:T(8,128)(2,1)} async-done(((bf16[1024,512]{0,1:T(8,128)(2,1)}), bf16[256,512]{0,1:T(8,128)(2,1)}) %reduce-scatter.23.cloned.1.call-update) | async-done | bytes 262160 | tf_op jit(solution)/shard_map/reduce_scatter | solution.py:385
  784.2 2.8 add_add_fusion.1
  792.5 3.4 add_add_fusion
  798.3 39.4 %all-reduce.14 = (f32[2048]{0:T(1024)S(1)}, f32[512]{0:T(512)S(1)}, f32[512]{0:T(512)S(1)}, f32[512]{0:T(512)S(1)}, f32[512]{0:T(512)S(1)}, /*index=5*/f32[512]{0:T(512)S(1)}, f32[512]{0:T(512)S(1)}) all-reduce(f32[2048]{0:T(1024)S(1)} %add_add_fusion.2, ...), channel_id=13, replica_groups=mesh['dp'=8,'fsdp'=4] {'dp','fsdp'}, use_global_device_ids=true, to_apply=%region_65.66.clone | all-reduce | flops 5120 | bytes 40960
  850.8 64.4 %reduce-scatter.25.cloned.1.call-done = f32[16,512]{1,0:T(8,128)} async-done(((f32[512,512]{1,0:T(8,128)}), f32[16,512]{1,0:T(8,128)}) %reduce-scatter.25.cloned.1.call-update) | async-done | bytes 32784 | tf_op jit(solution)/shard_map/reduce_scatter | solution.py:418
  915.2 135.1 %reduce-scatter.31.cloned.1.call-done = f32[16,512]{1,0:T(8,128)} async-done(((f32[512,512]{1,0:T(8,128)}), f32[16,512]{1,0:T(8,128)}) %reduce-scatter.31.cloned.1.call-update) | async-done | bytes 32784 | tf_op jit(solution)/shard_map/reduce_scatter | solution.py:421
  1050.3 134.4 %reduce-scatter.27.cloned.1.call-done = f32[16,512]{1,0:T(8,128)} async-done(((f32[512,512]{1,0:T(8,128)}), f32[16,512]{1,0:T(8,128)}) %reduce-scatter.27.cloned.1.call-update) | async-done | bytes 32784 | tf_op jit(solution)/shard_map/reduce_scatter | solution.py:419
  1184.7 134.7 %reduce-scatter.29.cloned.1.call-done = f32[16,512]{1,0:T(8,128)} async-done(((f32[512,512]{1,0:T(8,128)}), f32[16,512]{1,0:T(8,128)}) %reduce-scatter.29.cloned.1.call-update) | async-done | bytes 32784 | tf_op jit(solution)/shard_map/reduce_scatter | solution.py:420
  1319.4 148.2 %reduce-scatter.33.cloned.1.call-done = f32[16,2048]{1,0:T(8,128)} async-done(((f32[512,2048]{1,0:T(8,128)}), f32[16,2048]{1,0:T(8,128)}) %reduce-scatter.33.cloned.1.call-update) | async-done | bytes 131088 | tf_op jit(solution)/shard_map/reduce_scatter | solution.py:422
  1467.6 149.5 %reduce-scatter.35.cloned.1.call-done = f32[64,512]{1,0:T(8,128)} async-done(((f32[2048,512]{1,0:T(8,128)}), f32[64,512]{1,0:T(8,128)}) %reduce-scatter.35.cloned.1.call-update) | async-done | bytes 131088 | tf_op jit(solution)/shard_map/reduce_scatter | solution.py:424
  (799 shorter events, 296.6 us)
Async XLA Ops:
  7.2 359.6 %all-gather.9.cloned.1.call-start = ((), (), s32[]{:S(2)}) async-start(), calls=%async_computation.12 | async-start | bytes 1310720 | tf_op jit(solution)/shard_map/all_gather | solution.py:294
  81.5 77.2 %copy-start.1 = (bf16[512,512]{1,0:T(8,128)(2,1)}, bf16[512,512]{1,0:T(8,128)(2,1)S(1)}, u32[]{:S(2)}) copy-start(bf16[512,512]{1,0:T(8,128)(2,1)S(1)} %all_gather.38) | copy-start | bytes 1572868
  84.0 154.8 %copy-start.29 = (bf16[256,512]{1,0:T(8,128)(2,1)}, bf16[256,512]{1,0:T(8,128)(2,1)S(1)}, u32[]{:S(2)}) copy-start(bf16[256,512]{1,0:T(8,128)(2,1)S(1)} %get-tuple-element.1215) | copy-start | bytes 786436
  84.0 155.1 %copy-start.27 = (bf16[256,512]{1,0:T(8,128)(2,1)}, bf16[256,512]{1,0:T(8,128)(2,1)S(1)}, u32[]{:S(2)}) copy-start(bf16[256,512]{1,0:T(8,128)(2,1)S(1)} %get-tuple-element.1216) | copy-start | bytes 786436
  84.0 155.4 %copy-start.25 = (bf16[256,512]{1,0:T(8,128)(2,1)}, bf16[256,512]{1,0:T(8,128)(2,1)S(1)}, u32[]{:S(2)}) copy-start(bf16[256,512]{1,0:T(8,128)(2,1)S(1)} %get-tuple-element.1214) | copy-start | bytes 786436
  85.0 283.3 %all-gather.11.cloned.1.call-start = ((), (), s32[]{:S(2)}) async-start(), calls=%async_computation.13 | async-start | bytes 1310720 | tf_op jit(solution)/shard_map/all_gather | solution.py:293
  156.5 231.1 %all-gather.17.cloned.1.call-start = ((), (), s32[]{:S(2)}) async-start(), calls=%async_computation.16 | async-start | bytes 1310720 | tf_op jit(solution)/shard_map/all_gather | solution.py:294
  157.6 231.6 %all-gather.19.cloned.1.call-start = ((), (), s32[]{:S(2)}) async-start(), calls=%async_computation.17 | async-start | bytes 1310720 | tf_op jit(solution)/shard_map/all_gather | solution.py:293
  158.7 252.6 %all-gather.21.cloned.1.call-start = ((), (), s32[]{:S(2)}) async-start(), calls=%async_computation.18 | async-start | bytes 1310720 | tf_op jit(solution)/shard_map/all_gather | solution.py:294
  159.7 253.1 %all-gather.23.cloned.1.call-start = ((), (), s32[]{:S(2)}) async-start(), calls=%async_computation.19 | async-start | bytes 1310720 | tf_op jit(solution)/shard_map/all_gather | solution.py:293
  160.8 78.9 %copy-start.148 = (bf16[16]{0:T(256)(128)(2,1)S(1)}, bf16[16]{0:T(256)(128)(2,1)}, u32[]{:S(2)}) copy-start(bf16[16]{0:T(256)(128)(2,1)} %param.50) | copy-start | bytes 100
  160.8 79.2 %copy-start.149 = (bf16[16]{0:T(256)(128)(2,1)S(1)}, bf16[16]{0:T(256)(128)(2,1)}, u32[]{:S(2)}) copy-start(bf16[16]{0:T(256)(128)(2,1)} %param.49) | copy-start | bytes 100
  160.8 79.4 %copy-start.150 = (bf16[16]{0:T(256)(128)(2,1)S(1)}, bf16[16]{0:T(256)(128)(2,1)}, u32[]{:S(2)}) copy-start(bf16[16]{0:T(256)(128)(2,1)} %param.46) | copy-start | bytes 100
  160.8 79.7 %copy-start.151 = (bf16[16]{0:T(256)(128)(2,1)S(1)}, bf16[16]{0:T(256)(128)(2,1)}, u32[]{:S(2)}) copy-start(bf16[16]{0:T(256)(128)(2,1)} %param.48) | copy-start | bytes 100
  160.8 79.9 %copy-start.152 = (bf16[16]{0:T(256)(128)(2,1)S(1)}, bf16[16]{0:T(256)(128)(2,1)}, u32[]{:S(2)}) copy-start(bf16[16]{0:T(256)(128)(2,1)} %param.47) | copy-start | bytes 100
  160.8 80.1 %copy-start.153 = (bf16[16]{0:T(256)(128)(2,1)S(1)}, bf16[16]{0:T(256)(128)(2,1)}, u32[]{:S(2)}) copy-start(bf16[16]{0:T(256)(128)(2,1)} %param.51) | copy-start | bytes 100
  160.8 80.4 %copy-start.154 = (bf16[64]{0:T(256)(128)(2,1)S(1)}, bf16[64]{0:T(256)(128)(2,1)}, u32[]{:S(2)}) copy-start(bf16[64]{0:T(256)(128)(2,1)} %param.44) | copy-start | bytes 388
  160.9 120.0 %copy-start.146 = (s32[3,1,13]{2,1,0:T(1,128)S(1)}, s32[3,1,13]{2,1,0:T(1,128)}, u32[]{:S(2)}) copy-start(s32[3,1,13]{2,1,0:T(1,128)} %param.34) | copy-start | bytes 472
  160.9 278.7 %all-gather.13.cloned.1.call-start = ((), (), s32[]{:S(2)}) async-start(), calls=%async_computation.14 | async-start | bytes 2162688 | tf_op jit(solution)/shard_map/all_gather | solution.py:272
  161.6 281.7 %all-gather.15.cloned.1.call-start = ((), (), s32[]{:S(2)}) async-start(), calls=%async_computation.15 | async-start | bytes 2162688 | tf_op jit(solution)/shard_map/all_gather | solution.py:274
  162.4 515.5 %reduce-scatter.13.cloned.1.call-start = ((), (), s32[]{:S(2)}) async-start(), calls=%async_computation.20 | async-start | bytes 1310720 | tf_op jit(solution)/shard_map/reduce_scatter | solution.py:382
  280.2 176.8 %copy-start.91 = (f32[512]{0:T(512)}, f32[512]{0:T(512)S(1)}, u32[]{:S(2)}) copy-start(f32[512]{0:T(512)S(1)} %convert_element_type.345) | copy-start | bytes 6148
  280.2 178.2 %copy-start.83 = (f32[512]{0:T(512)}, f32[512]{0:T(512)S(1)}, u32[]{:S(2)}) copy-start(f32[512]{0:T(512)S(1)} %convert_element_type.344) | copy-start | bytes 6148
  282.4 82.4 %copy-start.143 = (f32[3,256]{1,0:T(4,128)S(1)}, f32[3,256]{1,0:T(4,128)}, u32[]{:S(2)}) copy-start(f32[3,256]{1,0:T(4,128)} %param.38) | copy-start | bytes 9220
  357.9 116.3 %copy-start.7 = (bf16[512,512]{1,0:T(8,128)(2,1)}, bf16[512,512]{1,0:T(8,128)(2,1)S(1)}, u32[]{:S(2)}) copy-start(bf16[512,512]{1,0:T(8,128)(2,1)S(1)} %all_gather.43) | copy-start | bytes 1572868
  533.2 147.0 %reduce-scatter.17.cloned.1.call-start = ((), (), s32[]{:S(2)}) async-start(), calls=%async_computation.22 | async-start | bytes 1310720 | tf_op jit(solution)/shard_map/reduce_scatter | solution.py:382
  536.2 73.4 %copy-start.8 = (bf16[512,512]{1,0:T(8,128)(2,1)S(1)}, bf16[512,512]{1,0:T(8,128)(2,1)}, u32[]{:S(2)}) copy-start(bf16[512,512]{1,0:T(8,128)(2,1)} %copy-done.7) | copy-start | bytes 1572868
  610.6 83.3 %reduce-scatter.21.cloned.1.call-start = ((), (), s32[]{:S(2)}) async-start(), calls=%async_computation.24 | async-start | bytes 1310720 | tf_op jit(solution)/shard_map/reduce_scatter | solution.py:382
  668.7 53.2 %reduce-scatter.15.cloned.1.call-start = ((), (), s32[]{:S(2)}) async-start(), calls=%async_computation.21 | async-start | bytes 1310720 | tf_op jit(solution)/shard_map/reduce_scatter | solution.py:385
  669.3 80.7 %reduce-scatter.19.cloned.1.call-start = ((), (), s32[]{:S(2)}) async-start(), calls=%async_computation.23 | async-start | bytes 1310720 | tf_op jit(solution)/shard_map/reduce_scatter | solution.py:385
  670.1 108.1 %reduce-scatter.23.cloned.1.call-start = ((), (), s32[]{:S(2)}) async-start(), calls=%async_computation.25 | async-start | bytes 1310720 | tf_op jit(solution)/shard_map/reduce_scatter | solution.py:385
  670.6 244.5 %reduce-scatter.25.cloned.1.call-start = ((), (), s32[]{:S(2)}) async-start(), calls=%async_computation.26 | async-start | bytes 1081344 | tf_op jit(solution)/shard_map/reduce_scatter | solution.py:418
  673.8 376.5 %reduce-scatter.31.cloned.1.call-start = ((), (), s32[]{:S(2)}) async-start(), calls=%async_computation.29 | async-start | bytes 1081344 | tf_op jit(solution)/shard_map/reduce_scatter | solution.py:421
  677.8 506.9 %reduce-scatter.27.cloned.1.call-start = ((), (), s32[]{:S(2)}) async-start(), calls=%async_computation.27 | async-start | bytes 1081344 | tf_op jit(solution)/shard_map/reduce_scatter | solution.py:419
  696.3 623.1 %reduce-scatter.29.cloned.1.call-start = ((), (), s32[]{:S(2)}) async-start(), calls=%async_computation.28 | async-start | bytes 1081344 | tf_op jit(solution)/shard_map/reduce_scatter | solution.py:420
  780.5 687.1 %reduce-scatter.33.cloned.1.call-start = ((), (), s32[]{:S(2)}) async-start(), calls=%async_computation.30 | async-start | bytes 4325376 | tf_op jit(solution)/shard_map/reduce_scatter | solution.py:422
  787.0 830.1 %reduce-scatter.35.cloned.1.call-start = ((), (), s32[]{:S(2)}) async-start(), calls=%async_computation.31 | async-start | bytes 4325376 | tf_op jit(solution)/shard_map/reduce_scatter | solution.py:424
  796.0 47.1 %copy-start.19 = (f32[256,512]{1,0:T(8,128)S(1)}, f32[256,512]{1,0:T(8,128)}, u32[]{:S(2)}) copy-start(f32[256,512]{1,0:T(8,128)} %copy-done.18) | copy-start | bytes 1572868
  796.0 47.1 %copy-start.21 = (f32[256,512]{1,0:T(8,128)S(1)}, f32[256,512]{1,0:T(8,128)}, u32[]{:S(2)}) copy-start(f32[256,512]{1,0:T(8,128)} %copy-done.20) | copy-start | bytes 1572868
  796.0 47.1 %copy-start.35 = (bf16[3,256,512]{2,1,0:T(8,128)(2,1)S(1)}, bf16[3,256,512]{2,1,0:T(8,128)(2,1)}, u32[]{:S(2)}) copy-start(bf16[3,256,512]{2,1,0:T(8,128)(2,1)} %param.32) | copy-start | bytes 2359300
  796.1 47.0 %copy-start.84 = (f32[512]{0:T(512)S(1)}, f32[512]{0:T(512)}, u32[]{:S(2)}) copy-start(f32[512]{0:T(512)} %copy-done.83) | copy-start | bytes 6148
  796.1 47.0 %copy-start.92 = (f32[512]{0:T(512)S(1)}, f32[512]{0:T(512)}, u32[]{:S(2)}) copy-start(f32[512]{0:T(512)} %copy-done.91) | copy-start | bytes 6148
  796.1 47.0 %copy-start.95 = (f32[256]{0:T(256)S(1)}, f32[256]{0:T(256)}, u32[]{:S(2)}) copy-start(f32[256]{0:T(256)} %copy-done.94) | copy-start | bytes 3076
  796.1 47.0 %copy-start.97 = (f32[256]{0:T(256)S(1)}, f32[256]{0:T(256)}, u32[]{:S(2)}) copy-start(f32[256]{0:T(256)} %copy-done.96) | copy-start | bytes 3076
  796.1 47.0 %copy-start.99 = (f32[256]{0:T(256)S(1)}, f32[256]{0:T(256)}, u32[]{:S(2)}) copy-start(f32[256]{0:T(256)} %copy-done.98) | copy-start | bytes 3076
  796.1 47.0 %copy-start.101 = (f32[256]{0:T(256)S(1)}, f32[256]{0:T(256)}, u32[]{:S(2)}) copy-start(f32[256]{0:T(256)} %copy-done.100) | copy-start | bytes 3076
  796.1 47.0 %copy-start.105 = (f32[256]{0:T(256)S(1)}, f32[256]{0:T(256)}, u32[]{:S(2)}) copy-start(f32[256]{0:T(256)} %copy-done.104) | copy-start | bytes 3076
  796.2 48.4 %copy-start.6 = (bf16[512,512]{1,0:T(8,128)(2,1)S(1)}, bf16[512,512]{1,0:T(8,128)(2,1)}, u32[]{:S(2)}) copy-start(bf16[512,512]{1,0:T(8,128)(2,1)} %copy-done.5) | copy-start | bytes 1572868
  (133 other events, 1066.3 us)
Sparse Core Ops, SparseCore 0:
  85.1 26.8 all-gather.8
  156.6 28.9 all-gather.10
  187.2 29.4 all-gather.16
  218.0 28.2 all-gather.18
  247.7 27.9 all-gather.20
  277.2 30.5 all-gather.22
  310.6 56.6 all-gather.12
  370.2 55.4 all-gather.14
  533.3 24.9 reduce-scatter.12
  610.7 24.9 reduce-scatter.16
  668.8 25.0 reduce-scatter.20
  696.1 25.7 reduce-scatter.14
  724.2 25.7 reduce-scatter.18
  752.3 25.7 reduce-scatter.22
  780.8 134.3 reduce-scatter.24
  918.0 132.3 reduce-scatter.30
  1053.0 131.6 reduce-scatter.26
  1187.5 131.8 reduce-scatter.28
  1322.2 145.3 reduce-scatter.32
  1470.3 146.7 reduce-scatter.34
where the time goes:
time: 1630 us; the launch traced here: 1620 us
  waiting for transfers between devices  860 us (53%)
  blocking collectives  372 us (23%)
  matrix products  205 us (13%)
  local copies, waits for them, and re-layouts  138 us (8%)
  other arithmetic  29.8 us (2%)
  between operations  16.7 us (1%)
    reduce_scatter x1, waiting for transfers between devices, per_device(): lax.psum_scatter(accum[6], ('dp', 'fsdp'), scatter_dimension=0, tiled=True)  150 us
    reduce_scatter x1, waiting for transfers between devices, per_device(): lax.psum_scatter(accum[4], ('dp', 'fsdp'), scatter_dimension=0, tiled=True)  148 us
    reduce_scatter x1, waiting for transfers between devices, per_device(): lax.psum_scatter(accum[3], ('dp', 'fsdp'), scatter_dimension=0, tiled=True)  135 us
    reduce_scatter x1, waiting for transfers between devices, per_device(): lax.psum_scatter(accum[2], ('dp', 'fsdp'), scatter_dimension=0, tiled=True)  135 us
    reduce_scatter x1, waiting for transfers between devices, per_device(): lax.psum_scatter(accum[1], ('dp', 'fsdp'), scatter_dimension=0, tiled=True)  134 us
    unnamed x2, blocking collectives  78.2 us
    reduce_scatter x3, waiting for transfers between devices, per_device(): lax.psum_scatter(grad_values_all.astype(jnp.bfloat16), 'fsdp', scatter_di...  77.9 us
    all_gather x1, blocking collectives, per_device(): lax.all_gather(w_query, ('dp', 'fsdp'), axis=0, tiled=True)  75.7 us
  transfers between devices with their start and end apart: 20, of which 10 were waited for; matrix products, arithmetic and copies ran while one was open for 17% of the time, Pallas kernels for 0%

commit v1 on v0

v1 whole, which is shorter than its diff:
```python
import functools
import math

import jax
import jax.numpy as jnp
from jax import lax
from jax.experimental import pallas as pl
from jax.experimental.pallas import tpu as pltpu
from jax.sharding import PartitionSpec as P

HEADS = 8
EPS = 1e-06
HALT_LIMIT = 0.99
GELU_C = math.sqrt(2.0 / math.pi)
GELU_A = 0.044715
LOG2E = 1.0 / math.log(2.0)
LN2 = math.log(2.0)
BIG = 2.0**100
F32 = jnp.float32
BF16 = jnp.bfloat16
MESH = pl.DeviceIdType.MESH
VECTORS = 6


def nn(a, b):
    return lax.dot_general(a, b, (((1,), (0,)), ((), ())), preferred_element_type=F32)


def nt(a, b):
    return lax.dot_general(a, b, (((1,), (1,)), ((), ())), preferred_element_type=F32)


def tn(a, b):
    return lax.dot_general(a, b, (((0,), (0,)), ((), ())), preferred_element_type=F32)


def iota(shape, axis):
    return lax.broadcasted_iota(jnp.int32, shape, axis)


def flip(index, bit):
    return index + bit - 2 * bit * lax.rem(lax.div(index, bit), 2)


def col_sum(values):
    return jnp.sum(values, axis=0, keepdims=True)


def norm(values):
    centered = values - jnp.mean(values, axis=-1, keepdims=True)
    inv = lax.rsqrt(jnp.mean(centered * centered, axis=-1, keepdims=True) + EPS)
    return centered * inv, inv


def norm_back(grad, normal, inv):
    return inv * (
        grad
        - jnp.mean(grad, axis=-1, keepdims=True)
        - normal * jnp.mean(grad * normal, axis=-1, keepdims=True)
    )


class Plan:
    def __init__(self, micro, rows, width, hidden, segs, n_dp, n_z, fused):
        self.micro, self.rows, self.width, self.hidden = micro, rows, width, hidden
        self.segs, self.n_dp, self.n_z, self.fused = segs, n_dp, n_z, fused
        self.tree = rows * n_z
        self.head = width // HEADS
        self.pair = 2 * self.head
        self.pairs = HEADS // 2
        self.cols = 4 * width + hidden
        self.devices = n_dp * n_z
        self.part = width // self.devices
        self.part_h = hidden // self.devices


def make_signal(p, sig):
    half = p.width // 2
    freq = jnp.exp(
        (-math.log(10000.0) / half) * iota((1, half), 1).astype(F32)
    )
    far = (iota((8, 1), 0) * p.rows).astype(F32) * freq
    far_sin, far_cos = jnp.sin(far), jnp.cos(far)
    step = 32

    @pl.loop(0, p.rows // step)
    def _(i):
        near = (iota((step, 1), 0) + i * step).astype(F32) * freq
        near_sin, near_cos = jnp.sin(near), jnp.cos(near)
        for b in range(p.n_z):
            s, c = far_sin[b : b + 1], far_cos[b : b + 1]
            at = pl.ds(pl.multiple_of(b * p.rows + i * step, step), step)
            sig[at, 0:half] = near_sin * c + near_cos * s
            sig[at, half : 2 * half] = near_cos * c - near_sin * s


def blocked_table(p, parent_row):
    size = 128
    up = jnp.where(
        iota((16, p.segs), 0) == parent_row, 1.0, 0.0
    )
    up = jnp.concatenate([up, jnp.zeros((16, size - p.segs), F32)], axis=1)
    up = jnp.concatenate([up, jnp.zeros((size - 16, size), F32)], axis=0)
    row, column = iota((size, size), 0), iota((size, size), 1)
    reach = jnp.where(row == column, 1.0, up)
    for _ in range(4):
        reach = jnp.minimum(nn(reach.astype(BF16), reach.astype(BF16)), 1.0)
    inside = (row < p.segs) & (column < p.segs)
    return jnp.where(inside & (reach < 0.5), -BIG, 0.0)


def prepare_micro(p, m, z, r):
    table = blocked_table(p, r.parent[pl.ds(m, 1), :])
    seg_row = r.seg[pl.ds(m, 1), :]
    hot = jnp.where(iota((128, p.tree), 0) == seg_row, 1.0, 0.0)
    r.kfull[:, 128:256] = hot.T.astype(BF16)
    own = pl.ds(pl.multiple_of(z * p.rows, p.rows), p.rows)
    hot = jnp.where(iota((128, p.rows), 0) == r.seg[pl.ds(m, 1), own], 1.0, 0.0)
    feature = nn(table.astype(BF16), hot.astype(BF16)).astype(BF16)
    r.qfull[128:256, 0 : p.rows] = feature
    r.qfull[128:256, p.rows : 2 * p.rows] = feature
    for b in range(p.n_z):
        at = slice(b * p.rows, (b + 1) * p.rows)
        r.h[at, :] = (r.states[m, b].astype(F32) + r.sig[at, :]).astype(BF16)

    w = p.width
    h_all = r.h[...]
    r.k[...] = nn(h_all, r.wa[:, w : 2 * w]).astype(BF16)
    r.v[...] = nn(h_all, r.wa[:, 2 * w : 3 * w]).astype(BF16)
    r.vt[...] = r.v[...].T
    q = nn(r.h[own, :], r.wa[:, 0:w]) * (LOG2E * p.head**-0.5)
    r.qt[...] = q.astype(BF16).T


def fill_pair(p, full, flat, i):
    low = pl.ds(pl.multiple_of(i * p.pair, p.pair), p.head)
    high = pl.ds(pl.multiple_of(i * p.pair + p.head, p.head), p.head)
    full[0 : p.head, 0 : p.rows] = flat[low, :].astype(BF16)
    full[p.head : p.pair, p.rows : 2 * p.rows] = flat[high, :].astype(BF16)


def attention_forward(p, r):
    @pl.loop(0, p.pairs)
    def _(i):
        lanes = pl.ds(pl.multiple_of(i * p.pair, p.pair), p.pair)
        r.kfull[:, 0:128] = r.k[:, lanes]
        fill_pair(p, r.qfull, r.qt, i)
        s = nn(r.kfull[...], r.qfull[...])
        top = jnp.max(s, axis=0, keepdims=True)
        r.e[i] = jnp.exp2(s - top).astype(BF16)
        r.vo[0:128, :] = r.vt[lanes, :]
        o = nn(r.vo[...], r.e[i])
        inv = 1.0 / o[128:136]
        r.inv[i] = inv
        low = pl.ds(pl.multiple_of(i * p.pair, p.pair), p.head)
        high = pl.ds(pl.multiple_of(i * p.pair + p.head, p.head), p.head)
        r.ot[low, :] = o[0 : p.head, 0 : p.rows] * inv[0:1, 0 : p.rows]
        r.ot[high, :] = o[p.head : p.pair, p.rows :] * inv[0:1, p.rows :]


def transition(p, m, z, r):
    w = p.width
    rows = p.rows
    vec = lambda k: r.vec[k : k + 1, :]
    gain_a, bias_a, gain_b, bias_b, halt_vec = vec(1), vec(2), vec(3), vec(4), vec(5)
    own = pl.ds(pl.multiple_of(z * rows, rows), rows)
    w_out = slice(3 * w, 4 * w)

    lane = iota((128, rows), 0)
    packed = jnp.where(
        lane == 0,
        r.halting[pl.ds(m, 1), :],
        jnp.where(lane == 1, r.ponder[pl.ds(m, 1), :], r.cot_halt[pl.ds(m, 1), :]),
    ).T
    halting, ponder, cot_halt = packed[:, 0:1], packed[:, 1:2], packed[:, 2:3]

    r.otb[...] = r.ot[...].astype(BF16)
    state = r.states[m, z].astype(F32)
    y1 = state + r.sig[own, :] + tn(r.otb[...], r.wa[:, w_out])
    xh1, inv1 = norm(y1)
    n1 = xh1 * gain_a + bias_a
    r.xh1[...] = xh1
    r.u[...] = n1.astype(BF16)
    r.acc[...] = n1

    @pl.loop(0, p.hidden // w)
    def _(j):
        at = pl.ds(pl.multiple_of(j * w, w), w)
        pre = nn(r.u[...], r.wa[:, pl.ds(pl.multiple_of(4 * w + j * w, w), w)])
        pre = pre + r.bup[:, at]
        square = pre * pre
        t = jnp.tanh(pre * (GELU_C + (GELU_C * GELU_A) * square))
        half = 0.5 + 0.5 * t
        f = (pre * half).astype(BF16)
        slope = half + (0.5 * pre) * (1.0 - t * t) * (
            GELU_C + (3.0 * GELU_A * GELU_C) * square
        )
        block = pl.ds(pl.multiple_of(j * rows, rows), rows)
        r.dkv[block, 0:w] = f
        r.dkv[block, w : 2 * w] = slope.astype(BF16)
        r.acc[...] += nn(f, r.wd[at, :])

    y2 = r.acc[...] + vec(0)
    xh2, inv2 = norm(y2)
    s2 = xh2 * gain_b + bias_b
    ph = jax.nn.sigmoid(jnp.sum(s2 * halt_vec, axis=1, keepdims=True))
    run = jnp.where(halting < HALT_LIMIT, 1.0, 0.0)
    room = run * (1.0 - halting)
    weight = room * ph
    state = r.states[m, z].astype(F32)
    r.new_state[m] = (weight * s2 + (1.0 - weight) * state).astype(BF16)
    lane = iota((rows, 128), 1)
    packed = jnp.where(
        lane == 0, halting + weight, ponder + run * (1.0 - weight)
    ).T
    r.new_halting[pl.ds(m, 1), :] = packed[0:1, :]
    r.new_ponder[pl.ds(m, 1), :] = packed[1:2, :]

    cot = r.cot[m].astype(F32)
    dw = jnp.sum(cot * (s2 - state), axis=1, keepdims=True) + cot_halt
    dl = dw * room * ph * (1.0 - ph)
    ds2 = weight * cot + dl * halt_vec
    r.gvec[5:6, :] += col_sum(dl * s2)
    r.gvec[3:4, :] += col_sum(ds2 * xh2)
    r.gvec[4:5, :] += col_sum(ds2)
    dy2 = norm_back(ds2 * gain_b, xh2, inv2)
    r.gvec[0:1, :] += col_sum(dy2)
    r.dg[...] = dy2.astype(BF16)
    r.acc[...] = dy2
    r.gstate[m] = (1.0 - weight) * cot

    @pl.loop(0, p.hidden // w)
    def _(j):
        at = pl.ds(pl.multiple_of(j * w, w), w)
        at_up = pl.ds(pl.multiple_of(4 * w + j * w, w), w)
        block = pl.ds(pl.multiple_of(j * rows, rows), rows)
        dz = nt(r.dg[...], r.wd[at, :]) * r.dkv[block, w : 2 * w].astype(F32)
        r.gbup[:, at] += col_sum(dz)
        dzb = dz.astype(BF16)
        r.acc[...] += nt(dzb, r.wa[:, at_up])
        r.ga[:, at_up] += tn(r.u[...], dzb)
        r.gd[at, :] += tn(r.dkv[block, 0:w], r.dg[...])

    dn1 = r.acc[...]
    xh1 = r.xh1[...]
    r.gvec[1:2, :] += col_sum(dn1 * xh1)
    r.gvec[2:3, :] += col_sum(dn1)
    dy1 = norm_back(dn1 * gain_a, xh1, inv1)
    r.gstate[m] += dy1
    da = dy1.astype(BF16)
    r.ga[:, w_out] += nn(r.otb[...], da)
    r.dot[...] = nt(r.wa[:, w_out], da)


def attention_backward(p, m, dp, z, r):
    w = p.width
    r.vt[...] = r.k[...].T

    @pl.loop(0, p.pairs)
    def _(i):
        lanes = pl.ds(pl.multiple_of(i * p.pair, p.pair), p.pair)
        low = pl.ds(pl.multiple_of(i * p.pair, p.pair), p.head)
        high = pl.ds(pl.multiple_of(i * p.pair + p.head, p.head), p.head)
        inv = r.inv[i]
        do_a = (r.dot[low, :] * inv[0:1, 0 : p.rows]).astype(BF16)
        do_b = (r.dot[high, :] * inv[0:1, p.rows :]).astype(BF16)
        r.dofull[0 : p.head, 0 : p.rows] = do_a
        r.dofull[p.head : p.pair, p.rows :] = do_b
        inner = jnp.concatenate(
            [
                col_sum(do_a.astype(F32) * r.ot[low, :]),
                col_sum(do_b.astype(F32) * r.ot[high, :]),
            ],
            axis=1,
        )
        rough = (-inner).astype(BF16).astype(F32)
        row = iota((16, 2 * p.rows), 0)
        r.dofull[128:144, :] = jnp.where(
            row == 0, rough, jnp.where(row == 1, -inner - rough, 0.0)
        ).astype(BF16)
        r.vfull[:, 0:128] = r.v[:, lanes]
        dp = nn(r.vfull[...], r.dofull[...])
        ds = (r.e[i].astype(F32) * dp).astype(BF16)
        r.ds[...] = ds
        fill_pair(p, r.qfull, r.qt, i)
        r.dkv[0 : p.tree, lanes] = (nt(ds, r.qfull[0:128, :]) * LN2).astype(BF16)
        r.dkv[0 : p.tree, pl.ds(pl.multiple_of(w + i * p.pair, p.pair), p.pair)] = nt(
            r.e[i], r.dofull[0:128, :]
        ).astype(BF16)
        dq = nn(r.vt[lanes, :], r.ds[...]) * (p.head**-0.5)
        r.dqt[low, :] = dq[0 : p.head, 0 : p.rows].astype(BF16)
        r.dqt[high, :] = dq[p.head : p.pair, p.rows :].astype(BF16)

    own = pl.ds(pl.multiple_of(z * p.rows, p.rows), p.rows)
    r.dq[...] = r.dqt[...].T
    r.gstate[m] += nt(r.dq[...], r.wa[:, 0:w])

    @pl.when(m >= 2)
    def _():
        for i in range(1, p.n_z):
            back_copy(p, m - 2, i, dp, z, r).wait_send()

    @pl.loop(0, p.n_z)
    def _(b):
        at = pl.ds(pl.multiple_of(b * p.rows, p.rows), p.rows)
        dh = nt(r.dkv[at, :], r.wa[:, w : 3 * w])
        r.dh[lax.rem(m, 2), b] = dh.astype(BF16)

        @pl.when(z == b)
        def _():
            r.gstate[m] += dh

    for i in range(1, p.n_z):
        back_copy(p, m, i, dp, z, r).start()

    r.ga[:, 0:w] += tn(r.h[own, :], r.dq[...])
    for j in range(2):
        at = slice(j * w, (j + 1) * w)
        to = slice((1 + j) * w, (2 + j) * w)
        r.ga[:, to] += tn(r.h[...], r.dkv[0 : p.tree, at])


def remote(src, dst, send, recv, device):
    return pltpu.make_async_remote_copy(
        src_ref=src,
        dst_ref=dst,
        send_sem=send,
        recv_sem=recv,
        device_id=device,
        device_id_type=MESH,
    )


def back_copy(p, m, i, dp, z, r):
    peer = lax.rem(z + i, p.n_z)
    return remote(
        r.dh.at[lax.rem(m, 2), peer],
        r.dh_in.at[m, i - 1],
        r.back_send.at[m, i - 1],
        r.back_recv.at[m, i - 1],
        (dp, peer),
    )


class Links:
    def __init__(self, send, recv):
        self.send, self.recv, self.used, self.sent = send, recv, 0, []

    def go(self, src, dst, device):
        copy = remote(src, dst, self.send.at[self.used], self.recv.at[self.used], device)
        self.used += 1
        copy.start()
        self.sent.append(copy)
        return copy

    def landed(self, copy):
        copy.wait_send()
        self.sent = [other for other in self.sent if other is not copy]

    def finish(self):
        for copy in self.sent:
            copy.wait_send()
        self.sent = []


def pieces(p, r):
    w = p.width
    return (
        (r.wa, p.part, 0, 3 * w),
        (r.wa, p.part, 3 * w, p.cols),
        (r.wd, p.part_h, 0, w),
        (r.ws, 16, 0, 128),
    )


def rows_of(dp, size):
    return pl.ds(pl.multiple_of(dp * size, size), size)


def gather_states_start(p, m, dp, z, r, links):
    copies = []
    for i in range(1, p.n_z):
        peer = lax.rem(z + i, p.n_z)
        copies.append(links.go(r.state.at[m], r.states.at[m, z], (dp, peer)))
    return copies


def gather_z_start(p, piece, dp, z, links):
    ref, part, c0, c1 = piece
    at = ref.at[rows_of(dp * p.n_z + z, part), c0:c1]
    return [links.go(at, at, (dp, lax.rem(z + i, p.n_z))) for i in range(1, p.n_z)]


def gather_rest(p, piece, dp, z, links):
    ref, part, c0, c1 = piece
    size = part * p.n_z
    mid = (c0 + c1) // 2 if c1 - c0 >= 256 else c1
    x, y, core = (flip(dp, 2), z), (flip(dp, 4), z), (flip(dp, 1), z)

    def send(block, a, b, to):
        at = ref.at[rows_of(block, size), a:b]
        return links.go(at, at, to)

    split = mid < c1
    dpx, dpy = flip(dp, 2), flip(dp, 4)
    dpxy = flip(dpx, 4)
    a1 = send(dp, c0, mid, x)
    b1 = send(dp, mid, c1, y) if split else None
    a2 = send(dp, c0, mid, y)
    b2 = send(dp, mid, c1, x) if split else None
    core0 = send(dp, c0, c1, core)
    a1.wait_recv()
    a3 = send(dpx, c0, mid, y)
    if split:
        b1.wait_recv()
        b3 = send(dpy, mid, c1, x)
        b2.wait_recv()
    core1 = send(dpx, c0, c1, core)
    a2.wait_recv()
    core2 = send(dpy, c0, c1, core)
    a3.wait_recv()
    if split:
        b3.wait_recv()
    core3 = send(dpxy, c0, c1, core)
    for copy in (core0, core1, core2, core3):
        copy.wait_recv()


def spread_vectors(p, r):
    r.wsf[...] = r.ws[...].astype(F32)

    def spread(k, part, total):
        g = r.wsf[pl.ds(k, p.devices, stride=16), :].astype(BF16)
        lane, column = iota((128, total), 0), iota((128, total), 1)
        place = jnp.where((lane < part) & (lax.rem(column, part) == lane), 1.0, 0.0)
        full = nn(g, place.astype(BF16))
        mine = lax.div(iota((p.devices, total), 1), part) == iota((p.devices, total), 0)
        return col_sum(jnp.where(mine, full, 0.0))

    for k in range(VECTORS):
        r.vec[k : k + 1, :] = spread(k, p.part, p.width)
    r.bup[...] = spread(VECTORS, p.part_h, p.hidden)


def collect_vectors(p, r):
    r.gs[...] = jnp.zeros(r.gs.shape, F32)

    def collect(k, row, part, total):
        mine = lax.div(iota((p.devices, total), 1), part) == iota((p.devices, total), 0)
        full = jnp.where(mine, row, 0.0)
        high = full.astype(BF16)
        rest = (full - high.astype(F32)).astype(BF16)
        lane, column = iota((128, total), 0), iota((128, total), 1)
        place = jnp.where(
            (lane < part) & (lax.rem(column, part) == lane), 1.0, 0.0
        ).astype(BF16)
        r.gs[pl.ds(k, p.devices, stride=16), :] = nt(high, place) + nt(rest, place)

    for k in range(VECTORS):
        collect(k, r.gvec[k : k + 1, :], p.part, p.width)
    collect(VECTORS, r.gbup[...], p.part_h, p.hidden)


def reduce_piece(p, g, part, c0, c1, bufs, dp, z, links):
    size = part * p.n_z
    cols = c1 - c0
    mid = cols // 2 if cols >= 256 else cols
    split = mid < cols
    s1, r1, r2, r3, s4, r4 = bufs
    s2 = s3 = s1
    x, y, core = (flip(dp, 2), z), (flip(dp, 4), z), (flip(dp, 1), z)
    dpx, dpy = flip(dp, 2), flip(dp, 4)
    order = (dp, dpx, dpy, flip(dpx, 4))
    links.finish()
    for k, block in enumerate(order):
        s1[k * size : (k + 1) * size, 0:cols] = g[
            rows_of(flip(block, 1), size), c0:c1
        ].astype(BF16)
    first = links.go(s1.at[:, 0:cols], r1.at[:, 0:cols], core)
    first.wait_recv()
    links.landed(first)
    for k, block in enumerate(order):
        g[rows_of(block, size), c0:c1] += r1[k * size : (k + 1) * size, 0:cols].astype(F32)

    def send2(slot, block, a, b):
        s2[slot * size : (slot + 1) * size, a:b] = g[
            rows_of(block, size), c0 + a : c0 + b
        ].astype(BF16)

    def add2(slot, block, a, b):
        g[rows_of(block, size), c0 + a : c0 + b] += r2[
            slot * size : (slot + 1) * size, a:b
        ].astype(F32)

    send2(0, order[1], 0, mid)
    send2(1, order[3], 0, mid)
    a1 = links.go(s2.at[0 : 2 * size, 0:mid], r2.at[:, 0:mid], x)
    if split:
        send2(0, order[2], mid, cols)
        send2(1, order[3], mid, cols)
        b1 = links.go(s2.at[0 : 2 * size, mid:cols], r2.at[:, mid:cols], y)
    a1.wait_recv()
    add2(0, order[0], 0, mid)
    add2(1, order[2], 0, mid)
    links.landed(a1)
    s3[0:size, 0:mid] = g[rows_of(order[2], size), c0 : c0 + mid].astype(BF16)
    a2 = links.go(s3.at[0:size, 0:mid], r3.at[:, 0:mid], y)
    if split:
        b1.wait_recv()
        add2(0, order[0], mid, cols)
        add2(1, order[1], mid, cols)
        links.landed(b1)
        s3[0:size, mid:cols] = g[rows_of(order[1], size), c0 + mid : c1].astype(BF16)
        b2 = links.go(s3.at[0:size, mid:cols], r3.at[:, mid:cols], x)
    a2.wait_recv()
    if split:
        b2.wait_recv()
    g[rows_of(dp, size), c0:c1] += r3[:, 0:cols].astype(F32)
    last = []
    for i in range(1, p.n_z):
        peer = lax.rem(z + i, p.n_z)
        s4[i - 1, :, 0:cols] = g[rows_of(dp * p.n_z + peer, part), c0:c1].astype(BF16)
        last.append(
            links.go(s4.at[i - 1, :, 0:cols], r4.at[i - 1, :, 0:cols], (dp, peer))
        )
    total = g[rows_of(dp * p.n_z + z, part), c0:c1]
    for i in range(1, p.n_z):
        last[i - 1].wait_recv()
        total = total + r4[i - 1, :, 0:cols].astype(F32)
    return total


class Refs:
    pass


def kernel(p, names, *refs):
    r = Refs()
    for name, ref in zip(names, refs):
        setattr(r, name, ref)
    dp = lax.axis_index("dp")
    z = lax.axis_index("fsdp")
    w = p.width
    links = Links(r.send_sem, r.recv_sem)

    barrier = pltpu.get_barrier_semaphore()
    peers = [(dp, lax.rem(z + i, p.n_z)) for i in range(1, p.n_z)]
    if p.fused:
        peers += [(flip(dp, bit), z) for bit in (1, 2, 4)]
        n = dp * p.n_z + z
        at = rows_of(n, p.part)
        r.wa[at, 0:w] = r.w_query[...]
        r.wa[at, w : 2 * w] = r.w_key[...]
        r.wa[at, 2 * w : 3 * w] = r.w_value[...]
        r.wa[at, 3 * w : 4 * w] = r.w_out[...]
        r.wa[at, 4 * w :] = r.w_up[...]
        r.wd[rows_of(n, p.part_h), :] = r.w_down[...]
        r.small[...] = jnp.zeros((16, 128), F32)
        for k, name in enumerate(
            ("b_down", "gain_one", "bias_one", "gain_two", "bias_two", "w_halt")
        ):
            r.small[k : k + 1, 0 : p.part] = getattr(r, name)[...].astype(F32)
        r.small[VECTORS : VECTORS + 1, 0 : p.part_h] = r.b_up[...].astype(F32)
        r.ws[rows_of(n, 16), :] = r.small[...].astype(BF16)
    for peer in peers:
        pl.semaphore_signal(barrier, inc=1, device_id=peer, device_id_type=MESH)
    pl.semaphore_wait(barrier, len(peers))

    coming = []
    if p.fused:
        stages = [gather_z_start(p, piece, dp, z, links) for piece in pieces(p, r)[:1]]
        coming += gather_states_start(p, 0, dp, z, r, links)
        stages += [gather_z_start(p, piece, dp, z, links) for piece in pieces(p, r)[1:]]
        for m in range(1, p.micro):
            coming += gather_states_start(p, m, dp, z, r, links)
    else:
        for m in range(p.micro):
            coming += gather_states_start(p, m, dp, z, r, links)

    for m in range(p.micro):
        r.states[m, z] = r.state[m]
    make_signal(p, r.sig)
    r.ga[...] = jnp.zeros(r.ga.shape, F32)
    r.gd[...] = jnp.zeros(r.gd.shape, F32)
    r.gvec[...] = jnp.zeros(r.gvec.shape, F32)
    r.gbup[...] = jnp.zeros(r.gbup.shape, F32)
    r.qfull[...] = jnp.zeros(r.qfull.shape, BF16)
    r.dofull[...] = jnp.zeros(r.dofull.shape, BF16)
    r.vo[128:144, :] = jnp.ones((16, p.tree), BF16)
    lane = iota((p.tree, 128), 1)
    r.vfull[:, 128:256] = jnp.where(lane < 2, 1.0, 0.0).astype(BF16)

    if p.fused:
        for piece, copies in zip(pieces(p, r), stages):
            for copy in copies:
                copy.wait_recv()
            gather_rest(p, piece, dp, z, links)
        spread_vectors(p, r)
    for copy in coming:
        copy.wait_recv()

    @pl.loop(0, p.micro)
    def _(m):
        prepare_micro(p, m, z, r)
        attention_forward(p, r)
        transition(p, m, z, r)
        attention_backward(p, m, dp, z, r)

    if p.fused:
        collect_vectors(p, r)
        bufs_f = [getattr(r, "f%d" % k) for k in range(6)]
        bufs = [r.f0] + [getattr(r, "b%d" % k) for k in range(1, 6)]
        bufs_d = [r.e.at[0]] + [getattr(r, "d%d" % k) for k in range(1, 6)]
        bufs_s = [getattr(r, "e%d" % k) for k in range(6)]
        total = reduce_piece(p, r.ga, p.part, 3 * w, p.cols, bufs_f, dp, z, links)
        r.g_out[...] = total[:, 0:w]
        r.g_up[...] = total[:, w:]
        r.g_down[...] = reduce_piece(p, r.gd, p.part_h, 0, w, bufs_d, dp, z, links)
        total = reduce_piece(p, r.ga, p.part, 0, 3 * w, bufs, dp, z, links)
        r.g_query[...] = total[:, 0:w]
        r.g_key[...] = total[:, w : 2 * w]
        r.g_value[...] = total[:, 2 * w : 3 * w]
        total = reduce_piece(p, r.gs, 16, 0, 128, bufs_s, dp, z, links)
        r.small[...] = total
        for k, name in enumerate(
            ("b_down", "gain_one", "bias_one", "gain_two", "bias_two", "w_halt")
        ):
            getattr(r, "g_" + name)[...] = r.small[k : k + 1, 0 : p.part]
        r.g_b_up[...] = r.small[VECTORS : VECTORS + 1, 0 : p.part_h]
    for m in range(p.micro):
        for i in range(1, p.n_z):
            copy = back_copy(p, m, i, dp, z, r)
            copy.wait_recv()
            if m >= p.micro - 2:
                copy.wait_send()
            r.gstate[m] += r.dh_in[m, i - 1].astype(F32)
    links.finish()


def run_kernel(p, inputs):
    w, t, rows = p.width, p.tree, p.rows
    outs = {
        "new_state": ((p.micro, rows, w), BF16),
        "new_halting": ((p.micro, rows), F32),
        "new_ponder": ((p.micro, rows), F32),
        "gstate": ((p.micro, rows, w), F32),
    }
    scratch = {}
    if p.fused:
        for name in ("query", "key", "value", "out"):
            outs["g_" + name] = ((p.part, w), F32)
        outs["g_up"] = ((p.part, p.hidden), F32)
        outs["g_down"] = ((p.part_h, w), F32)
        for name in ("b_down", "gain_one", "bias_one", "gain_two", "bias_two", "w_halt"):
            outs["g_" + name] = ((1, p.part), F32)
        outs["g_b_up"] = ((1, p.part_h), F32)
        scratch.update(
            wa=((w, p.cols), BF16),
            wd=((p.hidden, w), BF16),
            ws=((p.devices * 16, 128), BF16),
            wsf=((p.devices * 16, 128), F32),
            small=((16, 128), F32),
            vec=((8, w), F32),
            bup=((1, p.hidden), F32),
            ga=((w, p.cols), F32),
            gd=((p.hidden, w), F32),
            gs=((p.devices * 16, 128), F32),
            gvec=((8, w), F32),
            gbup=((1, p.hidden), F32),
        )
        kinds = (
            ("f", p.part, p.cols - 3 * w),
            ("b", p.part, 3 * w),
            ("d", p.part_h, w),
            ("e", 16, 128),
        )
        for tag, part, cols in kinds:
            size = part * p.n_z
            shapes = [(k * size, cols) for k in (4, 4, 2, 1)]
            shapes += [(p.n_z - 1, part, cols)] * 2
            for k, shape in enumerate(shapes):
                if k or tag in "fe":
                    scratch[tag + str(k)] = (shape, BF16)
    else:
        outs.update(
            ga=((w, p.cols), F32),
            gd=((p.hidden, w), F32),
            gvec=((8, w), F32),
            gbup=((1, p.hidden), F32),
        )
    scratch.update(
        states=((p.micro, p.n_z, rows, w), BF16),
        sig=((t, w), F32),
        h=((t, w), BF16),
        k=((t, w), BF16),
        v=((t, w), BF16),
        vt=((w, t), BF16),
        qt=((w, rows), BF16),
        kfull=((t, 256), BF16),
        qfull=((256, 2 * rows), BF16),
        vfull=((t, 256), BF16),
        dofull=((256, 2 * rows), BF16),
        vo=((144, t), BF16),
        e=((p.pairs, t, 2 * rows), BF16),
        inv=((p.pairs, 8, 2 * rows), F32),
        ot=((w, rows), F32),
        otb=((w, rows), BF16),
        dot=((w, rows), F32),
        xh1=((rows, w), F32),
        u=((rows, w), BF16),
        acc=((rows, w), F32),
        dg=((rows, w), BF16),
        ds=((t, 2 * rows), BF16),
        dkv=((max(t, rows * (p.hidden // w)), 2 * w), BF16),
        dqt=((w, rows), BF16),
        dq=((rows, w), BF16),
        dh=((2, p.n_z, rows, w), BF16),
        dh_in=((p.micro, p.n_z - 1, rows, w), BF16),
    )
    vmem = pl.BlockSpec(memory_space=pltpu.VMEM)
    copies = 128
    names = (
        list(inputs)
        + list(outs)
        + list(scratch)
        + ["send_sem", "recv_sem", "back_send", "back_recv"]
    )
    results = pl.pallas_call(
        functools.partial(kernel, p, names),
        out_shape=[jax.ShapeDtypeStruct(s, d) for s, d in outs.values()],
        in_specs=[vmem] * len(inputs),
        out_specs=[vmem] * len(outs),
        scratch_shapes=[pltpu.VMEM(s, d) for s, d in scratch.values()]
        + [pltpu.SemaphoreType.DMA((copies,))] * 2
        + [pltpu.SemaphoreType.DMA((p.micro, p.n_z - 1))] * 2,
        compiler_params=pltpu.CompilerParams(
            collective_id=0, has_side_effects=True, vmem_limit_bytes=62 << 20
        ),
        name="layer",
    )(*inputs.values())
    return dict(zip(outs, results))


WEIGHTS = (
    "w_query",
    "w_key",
    "w_value",
    "w_out",
    "w_up",
    "b_up",
    "w_down",
    "b_down",
    "gain_one",
    "bias_one",
    "gain_two",
    "bias_two",
    "w_halt",
)


def per_device(state, segment, parent, halting, ponder, cot_state, cot_halt, *weights):
    micro, rows, width = state.shape
    given = dict(zip(WEIGHTS, weights))
    n_dp, n_z = lax.axis_size("dp"), lax.axis_size("fsdp")
    part, hidden = given["w_query"].shape[0], given["w_up"].shape[1]
    fused = n_dp == 8 and part % 16 == 0 and part <= 128
    p = Plan(micro, rows, width, hidden, parent.shape[2], n_dp, n_z, fused)
    inputs = dict(
        state=state,
        seg=segment,
        parent=parent.reshape(micro, p.segs),
        halting=halting,
        ponder=ponder,
        cot=cot_state,
        cot_halt=cot_halt,
    )
    if fused:
        for name, value in given.items():
            inputs[name] = value if value.ndim == 2 else value.reshape(1, -1)
        out = run_kernel(p, inputs)
        grads = []
        for name in WEIGHTS:
            value = out["g_" + name[2:]] if name.startswith("w_") and name != "w_halt" else out["g_" + name]
            grads.append(value.reshape(given[name].shape))
    else:
        axes = ("dp", "fsdp")
        full = {k: lax.all_gather(v, axes, axis=0, tiled=True) for k, v in given.items()}
        inputs["wa"] = jnp.concatenate([full[k] for k in WEIGHTS[:5]], axis=1)
        inputs["wd"] = full["w_down"]
        rows_f32 = [full[k].astype(F32) for k in WEIGHTS[7:]]
        rows_f32 += [jnp.zeros((width,), F32)] * 2
        inputs["vec"] = jnp.stack(rows_f32)
        inputs["bup"] = full["b_up"].astype(F32).reshape(1, -1)
        out = run_kernel(p, inputs)
        whole = [out["ga"][:, k * width : (k + 1) * width] for k in range(4)]
        whole += [out["ga"][:, 4 * width :], out["gbup"][0], out["gd"]]
        whole += [out["gvec"][k] for k in range(VECTORS)]
        grads = [
            lax.psum_scatter(g, axes, scatter_dimension=0, tiled=True) for g in whole
        ]
    return (out["new_state"], out["new_halting"], out["new_ponder"], out["gstate"], *grads)


def solution(mesh):
    tokens, flags = P(None, ("dp", "fsdp"), None), P(None, ("dp", "fsdp"))
    matrix, vector = P(("dp", "fsdp"), None), P(("dp", "fsdp"))
    weights = tuple(
        matrix if name in ("w_query", "w_key", "w_value", "w_out", "w_up", "w_down") else vector
        for name in WEIGHTS
    )
    return jax.shard_map(
        per_device,
        mesh=mesh,
        in_specs=(tokens, P(None, "dp"), P(None, "dp", None), flags, flags, tokens, flags)
        + weights,
        out_specs=(tokens, flags, flags, tokens) + weights,
        check_vma=False,
    )
```

time: 1630 us -> 261 us (0.16)
  waiting for transfers between devices: 860 us -> 0 us
  blocking collectives: 372 us -> 0 us
  Pallas kernels: 0 us -> 247 us
  matrix products: 205 us -> 0 us
  local copies, waits for them, and re-layouts: 138 us -> 13.2 us
  other arithmetic: 29.8 us -> 0 us
    reduce_scatter x12 -> x0, waiting for transfers between devices: 856 us -> none  [the longest x1 150 us: per_device(): lax.psum_scatter(accum[6], ('dp', 'fsdp'), scatter_dimension=0, tiled=True)]
    all_gather x4 -> x0, blocking collectives: 294 us -> none  [the longest x1 75.7 us: per_device(): lax.all_gather(w_query, ('dp', 'fsdp'), axis=0, tiled=True)]
    pallas_call x0 -> x1, Pallas kernels: none -> 247 us  [run_kernel(): pl.pallas_call(functools.partial(kernel, p, names), out_shape=[jax.ShapeD...]
    dot_general x180 -> x0, matrix products: 205 us -> none  [the longest x12 37.1 us: one_pair(): jnp.einsum('hrk,khd->rhd', grad_scores, key_pair, preferred_element_type=...]
    unnamed x2 -> x0, blocking collectives: 78.2 us -> none
    dynamic_slice x87 -> x0, local copies, waits for them, and re-layouts: 67.3 us -> none  [the longest x24 23.6 us: one_pair(): lax.dynamic_slice_in_dim(keys_all, column, pair_width, 1)]
    dynamic_update_slice x36 -> x0, local copies, waits for them, and re-layouts: 24.9 us -> none  [the longest x12 13.8 us: one_pair(): lax.dynamic_update_slice_in_dim(grad_values, value_part.reshape(tree_len,...]
  transfers between devices with their start and end apart: 20 -> 0, of which waited for: 10 -> 0; matrix products, arithmetic and copies ran while one was open for 17% -> 0% of each run, Pallas kernels for 0% -> 0%
where the time goes in v1:
time: 261 us
  Pallas kernels  247 us (95%)
  local copies, waits for them, and re-layouts  13.2 us (5%)
    pallas_call x1, Pallas kernels, run_kernel(): pl.pallas_call(functools.partial(kernel, p, names), out_shape=[jax.ShapeD...  247 us
    unnamed x50, local copies, waits for them, and re-layouts  13.2 us

profile of v1, /device:TPU:0, one launch (start us, length us, event | category | flops | bytes accessed | tf_op | source)
XLA Modules:
  0.0 260.8 jit_solution(9099593515743751731)
XLA Ops:
  0.7 1.3 copy.39
  1.9 246.8 %layer.1 = (bf16[3,256,512]{2,1,0:T(8,128)(2,1)}, f32[3,256]{1,0:T(4,128)}, f32[3,256]{1,0:T(4,128)}, f32[3,256,512]{2,1,0:T(8,128)}, f32[16,512]{1,0:T(8,128)},...) custom-call(bf16[3,256,512]{2,1,0:T(8,128)(2,1)} %refs_0_.1, ...), custom_call_target="tpu_custom_call" | custom-call | tf_op jit(solution)/shard_map/layer/pallas_call | solution.py:728
  248.7 0.0 copy-start.8
  248.8 0.0 copy-start.7
  248.8 0.0 copy-start
  248.8 2.2 copy.57
  251.0 0.0 copy-done.8
  251.0 0.6 copy.58
  251.6 0.0 copy-done.7
  251.6 0.6 copy.59
  252.2 0.0 copy-done
  252.2 0.0 copy-start.3
  252.2 0.0 copy-start.2
  252.2 0.0 copy-start.15
  252.2 0.0 copy-start.1
  252.2 0.0 copy-start.14
  252.2 0.0 copy-start.13
  252.2 0.0 copy-start.12
  252.2 0.0 copy-start.11
  252.2 0.0 copy-start.10
  252.3 0.0 copy-start.9
  252.3 1.1 copy.60
  253.4 0.0 copy-done.6
  253.4 0.6 copy.61
  254.0 0.0 copy-done.5
  254.0 0.6 copy.62
  254.6 0.0 copy-done.4
  254.6 0.6 copy.63
  255.3 0.0 copy-done.3
  255.3 0.6 copy.64
  255.9 0.0 copy-done.2
  255.9 0.7 copy.65
  256.5 0.0 copy-done.15
  256.5 0.5 copy.66
  257.1 0.0 copy-done.1
  257.1 0.7 copy.67
  257.7 0.0 copy-done.14
  257.7 0.5 copy.68
  258.2 0.0 copy-done.13
  258.2 0.5 copy.69
  258.7 0.0 copy-done.12
  258.7 0.5 copy.70
  259.3 0.0 copy-done.11
  259.3 0.5 copy.71
  259.8 0.0 copy-done.10
  259.8 0.5 copy.72
  260.3 0.0 copy-done.9
  260.3 0.5 copy.73
  (3 shorter events, 0.0 us)
Async XLA Ops:
  248.7 2.2 copy-start.8
  248.8 2.8 %copy-start.7 = (f32[3,256]{1,0:T(4,128)S(1)}, f32[3,256]{1,0:T(4,128)}, u32[]{:S(2)}) copy-start(f32[3,256]{1,0:T(4,128)} %get-tuple-element.70) | copy-start | bytes 9220
  248.8 3.4 %copy-start = (f32[3,256,512]{2,1,0:T(8,128)S(1)}, f32[3,256,512]{2,1,0:T(8,128)}, u32[]{:S(2)}) copy-start(f32[3,256,512]{2,1,0:T(8,128)} %get-tuple-element.71) | copy-start | bytes 4718596
  252.2 1.3 copy-start.6
  252.2 1.9 copy-start.5
  252.2 2.5 copy-start.4
  252.2 3.1 %copy-start.3 = (f32[16,512]{1,0:T(8,128)S(1)}, f32[16,512]{1,0:T(8,128)}, u32[]{:S(2)}) copy-start(f32[16,512]{1,0:T(8,128)} %get-tuple-element.75) | copy-start | bytes 98308
  252.2 3.7 %copy-start.2 = (f32[16,2048]{1,0:T(8,128)S(1)}, f32[16,2048]{1,0:T(8,128)}, u32[]{:S(2)}) copy-start(f32[16,2048]{1,0:T(8,128)} %get-tuple-element.76) | copy-start | bytes 393220
  252.2 4.4 %copy-start.15 = (f32[1,64]{1,0:T(1,128)S(1)}, f32[1,64]{1,0:T(1,128)}, u32[]{:S(2)}) copy-start(f32[1,64]{1,0:T(1,128)} %get-tuple-element.43) | copy-start | bytes 772
  252.2 4.9 %copy-start.1 = (f32[64,512]{1,0:T(8,128)S(1)}, f32[64,512]{1,0:T(8,128)}, u32[]{:S(2)}) copy-start(f32[64,512]{1,0:T(8,128)} %get-tuple-element.78) | copy-start | bytes 393220
  252.2 5.5 %copy-start.14 = (f32[1,16]{1,0:T(1,128)S(1)}, f32[1,16]{1,0:T(1,128)}, u32[]{:S(2)}) copy-start(f32[1,16]{1,0:T(1,128)} %get-tuple-element.45) | copy-start | bytes 196
  252.2 6.0 %copy-start.13 = (f32[1,16]{1,0:T(1,128)S(1)}, f32[1,16]{1,0:T(1,128)}, u32[]{:S(2)}) copy-start(f32[1,16]{1,0:T(1,128)} %get-tuple-element.46) | copy-start | bytes 196
  252.2 6.5 %copy-start.12 = (f32[1,16]{1,0:T(1,128)S(1)}, f32[1,16]{1,0:T(1,128)}, u32[]{:S(2)}) copy-start(f32[1,16]{1,0:T(1,128)} %get-tuple-element.47) | copy-start | bytes 196
  252.2 7.0 %copy-start.11 = (f32[1,16]{1,0:T(1,128)S(1)}, f32[1,16]{1,0:T(1,128)}, u32[]{:S(2)}) copy-start(f32[1,16]{1,0:T(1,128)} %get-tuple-element.48) | copy-start | bytes 196
  252.2 7.5 %copy-start.10 = (f32[1,16]{1,0:T(1,128)S(1)}, f32[1,16]{1,0:T(1,128)}, u32[]{:S(2)}) copy-start(f32[1,16]{1,0:T(1,128)} %get-tuple-element.49) | copy-start | bytes 196
  252.3 8.0 %copy-start.9 = (f32[1,16]{1,0:T(1,128)S(1)}, f32[1,16]{1,0:T(1,128)}, u32[]{:S(2)}) copy-start(f32[1,16]{1,0:T(1,128)} %get-tuple-element.50) | copy-start | bytes 196

commit v2 on v1

v2 whole, which is shorter than its diff:
```python
import functools
import math

import jax
import jax.numpy as jnp
from jax import lax
from jax.experimental import pallas as pl
from jax.experimental.pallas import tpu as pltpu
from jax.sharding import PartitionSpec as P

HEADS = 8
EPS = 1e-06
HALT_LIMIT = 0.99
GELU_C = math.sqrt(2.0 / math.pi)
GELU_A = 0.044715
LOG2E = 1.0 / math.log(2.0)
LN2 = math.log(2.0)
BIG = 2.0**100
F32 = jnp.float32
BF16 = jnp.bfloat16
MESH = pl.DeviceIdType.MESH
SMALL = ("b_down", "gain_one", "bias_one", "gain_two", "bias_two", "w_halt")
VECTORS = len(SMALL)


def nn(a, b):
    return lax.dot_general(a, b, (((1,), (0,)), ((), ())), preferred_element_type=F32)


def nt(a, b):
    return lax.dot_general(a, b, (((1,), (1,)), ((), ())), preferred_element_type=F32)


def tn(a, b):
    return lax.dot_general(a, b, (((0,), (0,)), ((), ())), preferred_element_type=F32)


def iota(shape, axis):
    return lax.broadcasted_iota(jnp.int32, shape, axis)


def flip(index, bit):
    return index + bit - 2 * bit * lax.rem(lax.div(index, bit), 2)


def col_sum(values):
    return jnp.sum(values, axis=0, keepdims=True)


def norm(values):
    centered = values - jnp.mean(values, axis=-1, keepdims=True)
    inv = lax.rsqrt(jnp.mean(centered * centered, axis=-1, keepdims=True) + EPS)
    return centered * inv, inv


def norm_back(grad, normal, inv):
    return inv * (
        grad
        - jnp.mean(grad, axis=-1, keepdims=True)
        - normal * jnp.mean(grad * normal, axis=-1, keepdims=True)
    )


class Plan:
    def __init__(self, micro, rows, width, hidden, segs, n_dp, n_z, fused):
        self.micro, self.rows, self.width, self.hidden = micro, rows, width, hidden
        self.segs, self.n_dp, self.n_z, self.fused = segs, n_dp, n_z, fused
        self.tree = rows * n_z
        self.head = width // HEADS
        self.pair = 2 * self.head
        self.pairs = HEADS // 2
        self.cols = 4 * width + hidden
        self.devices = n_dp * n_z
        self.part = width // self.devices
        self.part_h = hidden // self.devices


def make_signal(p, r):
    half = p.width // 2
    freq = jnp.exp((-math.log(10000.0) / half) * iota((1, half), 1).astype(F32))
    far = (iota((8, 1), 0) * p.rows).astype(F32) * freq
    r.far[:, 0:half] = jnp.sin(far)
    r.far[:, half:] = jnp.cos(far)
    step = 32

    @pl.loop(0, p.rows // step)
    def _(i):
        near = (iota((step, 1), 0) + i * step).astype(F32) * freq
        at = pl.ds(pl.multiple_of(i * step, step), step)
        r.near[at, 0:half] = jnp.sin(near)
        r.near[at, half:] = jnp.cos(near)


def signal(p, r, b):
    half = p.width // 2
    far_sin, far_cos = r.far[pl.ds(b, 1), 0:half], r.far[pl.ds(b, 1), half:]
    near_sin, near_cos = r.near[:, 0:half], r.near[:, half:]
    return near_sin * far_cos + near_cos * far_sin, near_cos * far_cos - near_sin * far_sin


def blocked_table(p, parent_row):
    size = 128
    up = jnp.where(
        iota((16, p.segs), 0) == parent_row, 1.0, 0.0
    )
    up = jnp.concatenate([up, jnp.zeros((16, size - p.segs), F32)], axis=1)
    up = jnp.concatenate([up, jnp.zeros((size - 16, size), F32)], axis=0)
    row, column = iota((size, size), 0), iota((size, size), 1)
    reach = jnp.where(row == column, 1.0, up)
    for _ in range(4):
        reach = jnp.minimum(nn(reach.astype(BF16), reach.astype(BF16)), 1.0)
    inside = (row < p.segs) & (column < p.segs)
    return jnp.where(inside & (reach < 0.5), -BIG, 0.0)


def prepare_micro(p, m, z, r):
    table = blocked_table(p, r.parent[m])
    seg_row = r.seg[pl.ds(m, 1), :]
    hot = jnp.where(iota((128, p.tree), 0) == seg_row, 1.0, 0.0)
    r.kfull[:, 128:256] = hot.T.astype(BF16)
    own = pl.ds(pl.multiple_of(z * p.rows, p.rows), p.rows)
    hot = jnp.where(iota((128, p.rows), 0) == r.seg[pl.ds(m, 1), own], 1.0, 0.0)
    feature = nn(table.astype(BF16), hot.astype(BF16)).astype(BF16)
    r.qfull[128:256, 0 : p.rows] = feature
    r.qfull[128:256, p.rows : 2 * p.rows] = feature
    for b in range(p.n_z):
        at = slice(b * p.rows, (b + 1) * p.rows)
        for k, wave in enumerate(signal(p, r, b)):
            lanes = slice(k * (p.width // 2), (k + 1) * (p.width // 2))
            r.h[at, lanes] = (r.states[m, b, :, lanes].astype(F32) + wave).astype(BF16)

    w = p.width
    half = p.tree // 2
    for c in range(2):
        at = slice(c * half, (c + 1) * half)
        r.k[at, :] = nn(r.h[at, :], r.wa[:, w : 2 * w]).astype(BF16)
        r.v[at, :] = nn(r.h[at, :], r.wa[:, 2 * w : 3 * w]).astype(BF16)
    r.vt[...] = r.v[...].T
    q = nn(r.h[own, :], r.wa[:, 0:w]) * (LOG2E * p.head**-0.5)
    r.qt[...] = q.astype(BF16).T


def fill_pair(p, full, flat, i):
    low = pl.ds(pl.multiple_of(i * p.pair, p.pair), p.head)
    high = pl.ds(pl.multiple_of(i * p.pair + p.head, p.head), p.head)
    full[0 : p.head, 0 : p.rows] = flat[low, :].astype(BF16)
    full[p.head : p.pair, p.rows : 2 * p.rows] = flat[high, :].astype(BF16)


def attention_forward(p, r):
    step = p.tree // 8

    def ready(i):
        r.kfull[:, 0:128] = r.k[:, pl.ds(pl.multiple_of(i * p.pair, p.pair), p.pair)]
        fill_pair(p, r.qfull, r.qt, i)

    def scores(c, top):
        at = slice(c * step, (c + 1) * step)
        s = nn(r.kfull[at, :], r.qfull[...])
        r.s[at, :] = s
        own = jnp.max(s.reshape(step // 8, 8, 2 * p.rows), axis=0)
        return own if top is None else jnp.maximum(top, own)

    def soften(i, c, top):
        at = slice(c * step, (c + 1) * step)
        r.e[i, at, :] = jnp.exp2(r.s[at, :] - top).astype(BF16)

    def finish(i):
        lanes = pl.ds(pl.multiple_of(i * p.pair, p.pair), p.pair)
        r.vo[0:128, :] = r.vt[lanes, :]
        o = nn(r.vo[...], r.e[i])
        inv = 1.0 / o[128:136]
        r.inv[i] = inv
        low = pl.ds(pl.multiple_of(i * p.pair, p.pair), p.head)
        high = pl.ds(pl.multiple_of(i * p.pair + p.head, p.head), p.head)
        r.ot[low, :] = o[0 : p.head, 0 : p.rows] * inv[0:1, 0 : p.rows]
        r.ot[high, :] = o[p.head : p.pair, p.rows :] * inv[0:1, p.rows :]

    ready(0)
    top = None
    for c in range(8):
        top = scores(c, top)
    r.top[...] = top

    @pl.loop(0, p.pairs - 1)
    def _(i):
        ready(i + 1)
        top = jnp.max(r.top[...], axis=0, keepdims=True)
        later = None
        for c in range(8):
            soften(i, c, top)
            later = scores(c, later)
        r.top[...] = later
        finish(i)

    top = jnp.max(r.top[...], axis=0, keepdims=True)
    for c in range(8):
        soften(p.pairs - 1, c, top)
    finish(p.pairs - 1)


def transition(p, m, z, r, between):
    w = p.width
    rows = p.rows
    vec = lambda k: r.vec[k : k + 1, :]
    gain_a, bias_a, gain_b, bias_b, halt_vec = vec(1), vec(2), vec(3), vec(4), vec(5)
    w_out = slice(3 * w, 4 * w)

    lane = iota((128, rows), 0)
    packed = jnp.where(
        lane == 0,
        r.halting[pl.ds(m, 1), :],
        jnp.where(lane == 1, r.ponder[pl.ds(m, 1), :], r.cot_halt[pl.ds(m, 1), :]),
    ).T
    halting, ponder, cot_halt = packed[:, 0:1], packed[:, 1:2], packed[:, 2:3]

    r.otb[...] = r.ot[...].astype(BF16)
    state = r.states[m, z].astype(F32)
    y1 = state + jnp.concatenate(signal(p, r, z), axis=1) + tn(r.otb[...], r.wa[:, w_out])
    xh1, inv1 = norm(y1)
    n1 = xh1 * gain_a + bias_a
    r.xh1[...] = xh1
    r.u[...] = n1.astype(BF16)
    r.acc[...] = n1

    wide = w // 2
    count = p.hidden // wide

    def expand(c):
        r.pre[c % 2] = (
            nn(r.u[...], r.wa[:, 4 * w + c * wide : 4 * w + (c + 1) * wide])
            + r.bup[:, c * wide : (c + 1) * wide]
        )

    def bend(c):
        block = slice((c // 2) * rows, (c // 2 + 1) * rows)
        off = (c % 2) * wide
        pre = r.pre[c % 2]
        square = pre * pre
        t = jnp.tanh(pre * (GELU_C + (GELU_C * GELU_A) * square))
        half = 0.5 + 0.5 * t
        r.dkv[block, off : off + wide] = (pre * half).astype(BF16)
        slope = half + (0.5 * pre) * (1.0 - t * t) * (
            GELU_C + (3.0 * GELU_A * GELU_C) * square
        )
        r.dkv[block, w + off : w + off + wide] = slope.astype(BF16)

    def shrink(c):
        block = slice((c // 2) * rows, (c // 2 + 1) * rows)
        off = (c % 2) * wide
        r.acc[...] += nn(
            r.dkv[block, off : off + wide], r.wd[c * wide : (c + 1) * wide, :]
        )

    expand(0)
    for c in range(count):
        if c + 1 < count:
            expand(c + 1)
        bend(c)
        if c:
            shrink(c - 1)
    shrink(count - 1)

    between()
    y2 = r.acc[...] + vec(0)
    xh2, inv2 = norm(y2)
    s2 = xh2 * gain_b + bias_b
    ph = jax.nn.sigmoid(jnp.sum(s2 * halt_vec, axis=1, keepdims=True))
    run = jnp.where(halting < HALT_LIMIT, 1.0, 0.0)
    room = run * (1.0 - halting)
    weight = room * ph
    state = r.states[m, z].astype(F32)
    r.new_state[m] = (weight * s2 + (1.0 - weight) * state).astype(BF16)
    lane = iota((rows, 128), 1)
    packed = jnp.where(
        lane == 0, halting + weight, ponder + run * (1.0 - weight)
    ).T
    r.new_halting[pl.ds(m, 1), :] = packed[0:1, :]
    r.new_ponder[pl.ds(m, 1), :] = packed[1:2, :]

    cot = r.cot[m].astype(F32)
    dw = jnp.sum(cot * (s2 - state), axis=1, keepdims=True) + cot_halt
    dl = dw * room * ph * (1.0 - ph)
    ds2 = weight * cot + dl * halt_vec
    r.gvec[5:6, :] += col_sum(dl * s2)
    r.gvec[3:4, :] += col_sum(ds2 * xh2)
    r.gvec[4:5, :] += col_sum(ds2)
    dy2 = norm_back(ds2 * gain_b, xh2, inv2)
    r.gvec[0:1, :] += col_sum(dy2)
    r.dg[...] = dy2.astype(BF16)
    r.acc[...] = dy2
    r.gstate[m] = (1.0 - weight) * cot

    @pl.loop(0, p.hidden // w)
    def _(j):
        at = pl.ds(pl.multiple_of(j * w, w), w)
        at_up = pl.ds(pl.multiple_of(4 * w + j * w, w), w)
        block = pl.ds(pl.multiple_of(j * rows, rows), rows)
        dz = nt(r.dg[...], r.wd[at, :]) * r.dkv[block, w : 2 * w].astype(F32)
        r.gbup[:, at] += col_sum(dz)
        dzb = dz.astype(BF16)
        r.acc[...] += nt(dzb, r.wa[:, at_up])
        r.ga[:, at_up] += tn(r.u[...], dzb)
        r.gd[at, :] += tn(r.dkv[block, 0:w], r.dg[...])

    dn1 = r.acc[...]
    xh1 = r.xh1[...]
    r.gvec[1:2, :] += col_sum(dn1 * xh1)
    r.gvec[2:3, :] += col_sum(dn1)
    dy1 = norm_back(dn1 * gain_a, xh1, inv1)
    r.gstate[m] += dy1
    da = dy1.astype(BF16)
    r.ga[:, w_out] += nn(r.otb[...], da)
    r.dot[...] = nt(r.wa[:, w_out], da)


def attention_backward(p, r, inside):
    w = p.width

    @pl.loop(0, p.pairs)
    def _(i):
        inside(i)
        lanes = pl.ds(pl.multiple_of(i * p.pair, p.pair), p.pair)
        low = pl.ds(pl.multiple_of(i * p.pair, p.pair), p.head)
        high = pl.ds(pl.multiple_of(i * p.pair + p.head, p.head), p.head)
        inv = r.inv[i]
        do_a = (r.dot[low, :] * inv[0:1, 0 : p.rows]).astype(BF16)
        do_b = (r.dot[high, :] * inv[0:1, p.rows :]).astype(BF16)
        r.dofull[0 : p.head, 0 : p.rows] = do_a
        r.dofull[p.head : p.pair, p.rows :] = do_b
        inner = jnp.concatenate(
            [
                col_sum(do_a.astype(F32) * r.ot[low, :]),
                col_sum(do_b.astype(F32) * r.ot[high, :]),
            ],
            axis=1,
        )
        rough = (-inner).astype(BF16).astype(F32)
        row = iota((16, 2 * p.rows), 0)
        r.dofull[128:144, :] = jnp.where(
            row == 0, rough, jnp.where(row == 1, -inner - rough, 0.0)
        ).astype(BF16)
        r.vfull[:, 0:128] = r.v[:, lanes]
        fill_pair(p, r.qfull, r.qt, i)
        lanes_v = pl.ds(pl.multiple_of(w + i * p.pair, p.pair), p.pair)
        half = p.tree // 2
        for c in range(2):
            at = slice(c * half, (c + 1) * half)
            dp = nn(r.vfull[at, :], r.dofull[...])
            e = r.e[i, at, :]
            ds = (e.astype(F32) * dp).astype(BF16)
            r.ds[at, :] = ds
            r.dkv[at, lanes] = (nt(ds, r.qfull[0:128, :]) * LN2).astype(BF16)
            r.dkv[at, lanes_v] = nt(e, r.dofull[0:128, :]).astype(BF16)
        dq = nn(r.vt[lanes, :], r.ds[...]) * (p.head**-0.5)
        r.dqt[low, :] = dq[0 : p.head, 0 : p.rows].astype(BF16)
        r.dqt[high, :] = dq[p.head : p.pair, p.rows :].astype(BF16)


def back_to_input(p, m, z, r, back):
    w = p.width
    r.dq[...] = r.dqt[...].T
    r.gstate[m] += nt(r.dq[...], r.wa[:, 0:w])

    @pl.when(m >= 2)
    def _():
        back.left(m - 2)

    @pl.loop(0, p.n_z)
    def _(b):
        at = pl.ds(pl.multiple_of(b * p.rows, p.rows), p.rows)
        dh = nt(r.dkv[at, :], r.wa[:, w : 3 * w])
        r.dh[lax.rem(m, 2), b] = dh.astype(BF16)

        @pl.when(z == b)
        def _():
            r.gstate[m] += dh

    back.step(m, 0)


def input_gradients(p, z, r):
    w = p.width
    own = pl.ds(pl.multiple_of(z * p.rows, p.rows), p.rows)
    r.ga[:, 0:w] += tn(r.h[own, :], r.dq[...])
    for j in range(2):
        at = slice(j * w, (j + 1) * w)
        to = slice((1 + j) * w, (2 + j) * w)
        r.ga[:, to] += tn(r.h[...], r.dkv[0 : p.tree, at])


def remote(src, dst, send, recv, device):
    return pltpu.make_async_remote_copy(
        src_ref=src,
        dst_ref=dst,
        send_sem=send,
        recv_sem=recv,
        device_id=device,
        device_id_type=MESH,
    )


class Back:
    def __init__(self, p, dp, z, r):
        self.p, self.dp, self.z, self.r = p, dp, z, r
        self.last = p.n_z - 1

    def _copy(self, m, k, way, sender):
        r = self.r
        block = sender + way * (self.last - k)
        slot = block + 1 if way == 1 else block
        line = 0 if way == 1 else 1
        return remote(
            r.dh.at[lax.rem(m, 2), block],
            r.dh_in.at[m, slot],
            r.back_send.at[m, line, k],
            r.back_recv.at[m, line, k],
            (self.dp, sender + way),
        ), block, slot

    def _place(self, way):
        return self.z if way == 1 else self.last - self.z

    def step(self, m, k):
        r = self.r
        for way in (1, -1):
            place = self._place(way)
            if k == self.last:

                @pl.when(place > 0)
                def _():
                    copy, _, slot = self._copy(m, k - 1, way, self.z - way)
                    copy.wait_recv()
                    r.gstate[m] += r.dh_in[m, slot].astype(F32)

                continue

            @pl.when((place <= k) & (place < self.last))
            def _():
                if k:

                    @pl.when(place > 0)
                    def _():
                        copy, block, slot = self._copy(m, k - 1, way, self.z - way)
                        copy.wait_recv()
                        own = r.dh.at[lax.rem(m, 2), block]
                        own[...] = (
                            own[...].astype(F32) + r.dh_in[m, slot].astype(F32)
                        ).astype(BF16)

                self._copy(m, k, way, self.z)[0].start()

    def left(self, m):
        for way in (1, -1):
            place = self._place(way)
            for k in range(self.last):

                @pl.when((place <= k) & (place < self.last))
                def _():
                    self._copy(m, k, way, self.z)[0].wait_send()


class Copy:
    def __init__(self, flow, out, into=None, go=None, come=None):
        self.flow, self.out, self.into = flow, out, into or out
        self.go, self.come = go, come
        self.at = flow.used
        self.open = False
        flow.used += 1
        flow.copies.append(self)

    def _run(self, when, step):
        if when is None:
            step()
        else:
            pl.when(when())(step)

    def _make(self, ends):
        src, dst, device = ends()
        return remote(src, dst, self.flow.send.at[self.at], self.flow.recv.at[self.at], device)

    def start(self):
        self.open = True
        self._run(self.go, lambda: self._make(self.out).start())
        return self

    def arrived(self):
        self._run(self.come, lambda: self._make(self.into).wait_recv())

    def left(self):
        if self.open:
            self._run(self.go, lambda: self._make(self.out).wait_send())
            self.open = False


class Flow:
    def __init__(self, send, recv):
        self.send, self.recv, self.used, self.copies = send, recv, 0, []

    def finish(self):
        for copy in self.copies:
            copy.left()


class Line:
    def __init__(self, p, block, dp, z, flow):
        self.last = p.n_z - 1
        self.steps = []
        for step in range(p.n_z - 1):
            both = []
            for way in (1, -1):
                both.append(self._copy(p, block, dp, z, flow, step, way))
            self.steps.append(both)

    def _copy(self, p, block, dp, z, flow, step, way):
        place = z if way == 1 else self.last - z

        def out():
            at = block(z - way * step)
            return at, at, (dp, z + way)

        def into():
            at = block(z - way * (step + 1))
            return at, at, (dp, z - way)

        return Copy(
            flow,
            out,
            into,
            go=lambda: (place >= step) & (place < self.last),
            come=lambda: place >= step + 1,
        )

    def step(self, k):
        if k:
            for copy in self.steps[k - 1]:
                copy.arrived()
        if k < len(self.steps):
            for copy in self.steps[k]:
                copy.start()


def rows_of(dp, size):
    return pl.ds(pl.multiple_of(dp * size, size), size)


class Spread:
    def __init__(self, p, piece, dp, z, flow):
        ref, part, c0, c1 = piece
        size = part * p.n_z
        mid = (c0 + c1) // 2 if c1 - c0 >= 256 else c1
        self.split = mid < c1

        def made(block, turn, a, b):
            mine = ref.at[rows_of(block, size), a:b]
            theirs = ref.at[rows_of(flip(block, turn), size), a:b]
            to = (flip(dp, turn), z)
            return Copy(flow, lambda: (mine, mine, to), lambda: (theirs, theirs, to))

        dpx, dpy = flip(dp, 2), flip(dp, 4)
        dpxy = flip(dpx, 4)
        self.first = [made(dp, 2, c0, mid), made(dp, 4, c0, mid), made(dp, 1, c0, c1)]
        self.a3 = made(dpx, 4, c0, mid)
        if self.split:
            self.first += [made(dp, 4, mid, c1), made(dp, 2, mid, c1)]
            self.b3 = made(dpy, 2, mid, c1)
        self.cores = [made(block, 1, c0, c1) for block in (dpx, dpy, dpxy)]

    def start(self):
        for copy in self.first:
            copy.start()

    def middle(self):
        self.first[0].arrived()
        self.a3.start()
        if self.split:
            self.first[3].arrived()
            self.b3.start()
            self.first[4].arrived()
        self.cores[0].start()
        self.first[1].arrived()
        self.cores[1].start()

    def late(self):
        self.a3.arrived()
        if self.split:
            self.b3.arrived()
        self.cores[2].start()

    def end(self):
        self.first[2].arrived()
        for copy in self.cores:
            copy.arrived()


class Reduce:
    def __init__(self, p, g, part, c0, c1, bufs, dp, z, flow):
        self.p, self.g, self.part, self.c0, self.c1 = p, g, part, c0, c1
        self.dp, self.z = dp, z
        self.size = size = part * p.n_z
        self.cols = cols = c1 - c0
        self.mid = mid = cols // 2 if cols >= 256 else cols
        self.split = mid < cols
        self.s1, self.r1, self.r2, self.r3, self.s4, self.r4 = bufs
        s1, r1, r2, r3, s4, r4 = bufs
        x, y, core = (flip(dp, 2), z), (flip(dp, 4), z), (flip(dp, 1), z)
        dpx, dpy = flip(dp, 2), flip(dp, 4)
        self.order = (dp, dpx, dpy, flip(dpx, 4))

        def made(src, dst, to):
            return Copy(flow, lambda: (src, dst, to))

        self.core = made(s1.at[:, 0:cols], r1.at[:, 0:cols], core)
        self.a1 = made(s1.at[0 : 2 * size, 0:mid], r2.at[:, 0:mid], x)
        self.a2 = made(s1.at[0:size, 0:mid], r3.at[:, 0:mid], y)
        if self.split:
            self.b1 = made(s1.at[0 : 2 * size, mid:cols], r2.at[:, mid:cols], y)
            self.b2 = made(s1.at[0:size, mid:cols], r3.at[:, mid:cols], x)
        self.zs = []
        for i in range(1, p.n_z):
            peer = lax.rem(z + i, p.n_z)
            self.zs.append(made(s4.at[i - 1, :, 0:cols], r4.at[i - 1, :, 0:cols], (dp, peer)))

    def _rows(self, block, a, b):
        return self.g.at[rows_of(block, self.size), self.c0 + a : self.c0 + b]

    def _put(self, slot, block, a, b):
        size = self.size
        self.s1[slot * size : (slot + 1) * size, a:b] = self._rows(block, a, b)[...].astype(BF16)

    def _add(self, buf, slot, block, a, b):
        size = self.size
        self._rows(block, a, b)[...] += buf[slot * size : (slot + 1) * size, a:b].astype(F32)

    def core_start(self):
        for k, block in enumerate(self.order):
            self._put(k, flip(block, 1), 0, self.cols)
        self.core.start()

    def core_end(self):
        order, mid, cols = self.order, self.mid, self.cols
        self.core.arrived()
        self.core.left()
        for k, block in ((1, order[1]), (3, order[3])):
            self._add(self.r1, k, block, 0, mid)
        self._put(0, order[1], 0, mid)
        self._put(1, order[3], 0, mid)
        self.a1.start()
        if self.split:
            for k, block in ((2, order[2]), (3, order[3])):
                self._add(self.r1, k, block, mid, cols)
            self._put(0, order[2], mid, cols)
            self._put(1, order[3], mid, cols)
            self.b1.start()
            for k, block in ((0, order[0]), (1, order[1])):
                self._add(self.r1, k, block, mid, cols)
        for k, block in ((0, order[0]), (2, order[2])):
            self._add(self.r1, k, block, 0, mid)

    def plane_middle(self):
        order, mid, cols = self.order, self.mid, self.cols
        self.a1.arrived()
        self._add(self.r2, 1, order[2], 0, mid)
        self.a1.left()
        self._put(0, order[2], 0, mid)
        self.a2.start()
        self._add(self.r2, 0, order[0], 0, mid)
        if self.split:
            self.b1.arrived()
            self._add(self.r2, 1, order[1], mid, cols)
            self.b1.left()
            self._put(0, order[1], mid, cols)
            self.b2.start()
            self._add(self.r2, 0, order[0], mid, cols)

    def plane_end(self):
        self.a2.arrived()
        if self.split:
            self.b2.arrived()
        self._add(self.r3, 0, self.dp, 0, self.cols)
        p, part = self.p, self.part
        for i in range(1, p.n_z):
            peer = lax.rem(self.z + i, p.n_z)
            self.s4[i - 1, :, 0 : self.cols] = self.g[
                rows_of(self.dp * p.n_z + peer, part), self.c0 : self.c1
            ].astype(BF16)
            self.zs[i - 1].start()

    def total(self):
        p = self.p
        total = self.g[rows_of(self.dp * p.n_z + self.z, self.part), self.c0 : self.c1]
        for i in range(1, p.n_z):
            self.zs[i - 1].arrived()
            total = total + self.r4[i - 1, :, 0 : self.cols].astype(F32)
        return total


def spread_vectors(p, r):
    r.wsf[...] = r.ws[...].astype(F32)

    def spread(k, part, total):
        g = r.wsf[pl.ds(k, p.devices, stride=16), :].astype(BF16)
        lane, column = iota((128, total), 0), iota((128, total), 1)
        place = jnp.where((lane < part) & (lax.rem(column, part) == lane), 1.0, 0.0)
        full = nn(g, place.astype(BF16))
        mine = lax.div(iota((p.devices, total), 1), part) == iota((p.devices, total), 0)
        return col_sum(jnp.where(mine, full, 0.0))

    for k in range(VECTORS):
        r.vec[k : k + 1, :] = spread(k, p.part, p.width)
    r.bup[...] = spread(VECTORS, p.part_h, p.hidden)


def collect_vectors(p, r):
    r.gs[...] = jnp.zeros(r.gs.shape, F32)

    def collect(k, row, part, total):
        mine = lax.div(iota((p.devices, total), 1), part) == iota((p.devices, total), 0)
        full = jnp.where(mine, row, 0.0)
        high = full.astype(BF16)
        rest = (full - high.astype(F32)).astype(BF16)
        lane, column = iota((128, total), 0), iota((128, total), 1)
        place = jnp.where(
            (lane < part) & (lax.rem(column, part) == lane), 1.0, 0.0
        ).astype(BF16)
        r.gs[pl.ds(k, p.devices, stride=16), :] = nt(high, place) + nt(rest, place)

    for k in range(VECTORS):
        collect(k, r.gvec[k : k + 1, :], p.part, p.width)
    collect(VECTORS, r.gbup[...], p.part_h, p.hidden)


class Refs:
    pass


def buffers(r, tag):
    return [getattr(r, tag + str(k)) for k in range(6) if hasattr(r, tag + str(k))]


def targets(p, n, z, r):
    w = p.width
    at = rows_of(n, p.part)
    places = {}
    if p.fused:
        places["w_query"] = r.wa.at[at, 0:w]
        places["w_key"] = r.wa.at[at, w : 2 * w]
        places["w_value"] = r.wa.at[at, 2 * w : 3 * w]
        places["w_out"] = r.wa.at[at, 3 * w : 4 * w]
        places["w_up"] = r.wa.at[at, 4 * w :]
        places["w_down"] = r.wd.at[rows_of(n, p.part_h), :]
    places["state"] = r.states.at[:, z]
    return places


def place_vectors(p, n, r):
    r.small[...] = jnp.zeros((16, 128), F32)
    for k, name in enumerate(SMALL):
        r.small[k : k + 1, 0 : p.part] = getattr(r, name)[...].astype(F32)
    r.small[VECTORS : VECTORS + 1, 0 : p.part_h] = r.b_up[...].astype(F32)
    r.ws[rows_of(n, 16), :] = r.small[...].astype(BF16)


def clear(p, r):
    r.ga[...] = jnp.zeros(r.ga.shape, F32)
    r.gd[...] = jnp.zeros(r.gd.shape, F32)
    r.gvec[...] = jnp.zeros(r.gvec.shape, F32)
    r.gbup[...] = jnp.zeros(r.gbup.shape, F32)
    r.qfull[...] = jnp.zeros(r.qfull.shape, BF16)
    r.dofull[...] = jnp.zeros(r.dofull.shape, BF16)
    r.vo[128:144, :] = jnp.ones((16, p.tree), BF16)
    lane = iota((p.tree, 128), 1)
    r.vfull[:, 128:256] = jnp.where(lane < 2, 1.0, 0.0).astype(BF16)


def kernel(p, names, given, results, *refs):
    r = Refs()
    for name, ref in zip(names, refs):
        setattr(r, name, ref)
    dp = lax.axis_index("dp")
    z = lax.axis_index("fsdp")
    w = p.width
    places = targets(p, dp * p.n_z + z, z, r)
    loads = {}
    for k, name in enumerate(given):
        place = places.get(name, getattr(r, name, None))
        copy = pltpu.make_async_copy(getattr(r, "hbm_" + name), place, r.load_sem.at[k])
        loads[name] = copy
    stores = {}
    for k, name in enumerate(results):
        if name == "new_state":
            continue
        stores[name] = pltpu.make_async_copy(
            getattr(r, name), getattr(r, "hbm_" + name), r.store_sem.at[k]
        )
    flow = Flow(r.send_sem, r.recv_sem)

    barrier = pltpu.get_barrier_semaphore()
    peers = [(dp, lax.rem(z + i, p.n_z)) for i in range(1, p.n_z)]
    if p.fused:
        peers += [(flip(dp, bit), z) for bit in (1, 2, 4)]
    for peer in peers:
        pl.semaphore_signal(barrier, inc=1, device_id=peer, device_id_type=MESH)
    for copy in loads.values():
        copy.start()
    lines = [
        Line(p, lambda b, m=m: r.states.at[m, b], dp, z, flow) for m in range(p.micro)
    ]
    steps = p.n_z - 1
    back = Back(p, dp, z, r)
    if p.fused:
        parts = (
            (r.wa, p.part, 0, 3 * w),
            (r.ws, 16, 0, 128),
            (r.wa, p.part, 3 * w, p.cols),
            (r.wd, p.part_h, 0, w),
        )
        rods = []
        for ref, part, c0, c1 in parts:

            def block(b, ref=ref, part=part, c0=c0, c1=c1):
                return ref.at[rows_of(dp * p.n_z + b, part), c0:c1]

            rods.append(Line(p, block, dp, z, flow))
        spreads = [Spread(p, piece, dp, z, flow) for piece in parts]
        sums = [
            Reduce(p, r.ga, p.part, 3 * w, p.cols, buffers(r, "f"), dp, z, flow),
            Reduce(p, r.gd, p.part_h, 0, w, [r.k] + buffers(r, "d"), dp, z, flow),
            Reduce(p, r.gs, 16, 0, 128, buffers(r, "e"), dp, z, flow),
            Reduce(p, r.ga, p.part, 0, 3 * w, [r.q0] + buffers(r, "b"), dp, z, flow),
        ]
    for copy in loads.values():
        copy.wait()
    if p.fused:
        place_vectors(p, dp * p.n_z + z, r)
    pl.semaphore_wait(barrier, len(peers))

    if p.fused:
        for rod in rods:
            rod.step(0)
        make_signal(p, r)
        for k in range(1, steps):
            for rod in rods:
                rod.step(k)
            lines[0].step(k - 1)
            if k == 1:
                clear(p, r)
        for rod, spread in zip(rods, spreads):
            rod.step(steps)
            spread.start()
        lines[0].step(steps - 1)
        for spread in spreads:
            spread.middle()
        spreads[0].late()
        spreads[0].end()
        lines[0].step(steps)
        if p.micro > 1:
            lines[1].step(0)
    else:
        for k in range(steps + 1):
            for line in lines:
                line.step(k)
        make_signal(p, r)
        clear(p, r)

    @pl.loop(0, p.micro)
    def _(m):
        if p.fused:
            for k in range(1, p.micro):

                @pl.when(m == k)
                def _(k=k):
                    lines[k].step(steps)

        prepare_micro(p, m, z, r)
        if p.fused:

            @pl.when(m == 0)
            def _():
                for spread in spreads[1:]:
                    spread.late()

        attention_forward(p, r)

        @pl.when(m > 0)
        def _():
            for k in range(1, steps - 1):
                back.step(m - 1, k)

        if p.fused:

            @pl.when(m == 1)
            def _():
                for line in lines[2:]:
                    line.step(steps - 1)

            @pl.when(m == 0)
            def _():
                if p.micro > 1:
                    for k in range(1, steps - 1):
                        lines[1].step(k)
                for spread in spreads[1:]:
                    spread.end()
                spread_vectors(p, r)

        def between():
            if p.fused:

                @pl.when(m == 0)
                def _():
                    for line in lines[2:]:
                        line.step(0)

        transition(p, m, z, r, between)

        @pl.when(m > 0)
        def _():
            back.step(m - 1, steps - 1)

        out = pltpu.make_async_copy(
            r.new_state.at[m], r.hbm_new_state.at[m], r.state_sem.at[m]
        )
        out.start()
        if p.fused and p.micro > 1:

            @pl.when(m == 0)
            def _():
                lines[1].step(steps - 1)

        r.vt[...] = r.k[...].T
        if p.fused:

            @pl.when(m == p.micro - 1)
            def _():
                sums[0].core_start()
                sums[1].core_start()
                collect_vectors(p, r)
                sums[2].core_start()

        def inside(i):
            if p.fused:

                @pl.when((m == p.micro - 1) & (i == p.pairs // 2))
                def _():
                    for one in sums[:3]:
                        one.core_end()

        attention_backward(p, r, inside)
        if p.fused:

            @pl.when(m == 0)
            def _():
                for line in lines[2:]:
                    for k in range(1, steps - 1):
                        line.step(k)


        @pl.when(m > 0)
        def _():
            back.step(m - 1, steps)

        back_to_input(p, m, z, r, back)
        input_gradients(p, z, r)

    if p.fused:
        sums[3].core_start()
        for one in sums[:3]:
            one.plane_middle()
        sums[3].core_end()
        back.step(p.micro - 1, 1)
        for one in sums[:3]:
            one.plane_end()
        back.step(p.micro - 1, 2)
        sums[3].plane_middle()
        sums[3].plane_end()
        for k in range(3, steps + 1):
            back.step(p.micro - 1, k)
        total = sums[0].total()
        r.g_out[...] = total[:, 0:w]
        r.g_up[...] = total[:, w:]
        r.g_down[...] = sums[1].total()
        r.small[...] = sums[2].total()
        for k, name in enumerate(SMALL):
            getattr(r, "g_" + name)[...] = r.small[k : k + 1, 0 : p.part]
        r.g_b_up[...] = r.small[VECTORS : VECTORS + 1, 0 : p.part_h]
        total = sums[3].total()
        r.g_query[...] = total[:, 0:w]
        r.g_key[...] = total[:, w : 2 * w]
        r.g_value[...] = total[:, 2 * w : 3 * w]
    else:
        for k in range(1, steps + 1):
            back.step(p.micro - 1, k)
    for m in range(max(p.micro - 2, 0), p.micro):
        back.left(m)
    for copy in stores.values():
        copy.start()
    for m in range(p.micro):
        pltpu.make_async_copy(
            r.new_state.at[m], r.hbm_new_state.at[m], r.state_sem.at[m]
        ).wait()
    for copy in stores.values():
        copy.wait()
    flow.finish()


def run_kernel(p, inputs):
    w, t, rows = p.width, p.tree, p.rows
    outs = {
        "new_state": ((p.micro, rows, w), BF16),
        "new_halting": ((p.micro, rows), F32),
        "new_ponder": ((p.micro, rows), F32),
        "gstate": ((p.micro, rows, w), F32),
    }
    scratch = {}
    if p.fused:
        for name in ("query", "key", "value", "out"):
            outs["g_" + name] = ((p.part, w), F32)
        outs["g_up"] = ((p.part, p.hidden), F32)
        outs["g_down"] = ((p.part_h, w), F32)
        for name in SMALL:
            outs["g_" + name] = ((1, p.part), F32)
        outs["g_b_up"] = ((1, p.part_h), F32)
        scratch.update(
            wa=((w, p.cols), BF16),
            wd=((p.hidden, w), BF16),
            ws=((p.devices * 16, 128), BF16),
            wsf=((p.devices * 16, 128), F32),
            small=((16, 128), F32),
            vec=((8, w), F32),
            bup=((1, p.hidden), F32),
            ga=((w, p.cols), F32),
            gd=((p.hidden, w), F32),
            gs=((p.devices * 16, 128), F32),
            gvec=((8, w), F32),
            gbup=((1, p.hidden), F32),
        )
        kinds = (
            ("f", p.part, p.cols - 3 * w),
            ("b", p.part, 3 * w),
            ("d", p.part_h, w),
            ("e", 16, 128),
        )
        for tag, part, cols in kinds:
            size = part * p.n_z
            shapes = [(k * size, cols) for k in (4, 4, 2, 1)]
            shapes += [(p.n_z - 1, part, cols)] * 2
            for k, shape in enumerate(shapes):
                if k or tag in "fe":
                    scratch[tag + str(k)] = (shape, BF16)
        scratch["q0"] = ((4 * p.part * p.n_z, 3 * w), BF16)
    else:
        outs.update(
            ga=((w, p.cols), F32),
            gd=((p.hidden, w), F32),
            gvec=((8, w), F32),
            gbup=((1, p.hidden), F32),
        )
    scratch.update(
        states=((p.micro, p.n_z, rows, w), BF16),
        near=((rows, w), F32),
        far=((8, w), F32),
        h=((t, w), BF16),
        k=((t, w), BF16),
        v=((t, w), BF16),
        vt=((w, t), BF16),
        qt=((w, rows), BF16),
        kfull=((t, 256), BF16),
        qfull=((256, 2 * rows), BF16),
        vfull=((t, 256), BF16),
        dofull=((256, 2 * rows), BF16),
        vo=((144, t), BF16),
        e=((p.pairs, t, 2 * rows), BF16),
        s=((t, 2 * rows), F32),
        top=((8, 2 * rows), F32),
        pre=((2, rows, w // 2), F32),
        inv=((p.pairs, 8, 2 * rows), F32),
        ot=((w, rows), F32),
        otb=((w, rows), BF16),
        dot=((w, rows), F32),
        xh1=((rows, w), F32),
        u=((rows, w), BF16),
        acc=((rows, w), F32),
        dg=((rows, w), BF16),
        ds=((t, 2 * rows), BF16),
        dkv=((max(t, rows * (p.hidden // w)), 2 * w), BF16),
        dqt=((w, rows), BF16),
        dq=((rows, w), BF16),
        dh=((2, p.n_z, rows, w), BF16),
        dh_in=((p.micro, p.n_z + 1, rows, w), BF16),
    )
    direct = ("w_query", "w_key", "w_value", "w_out", "w_up", "w_down", "state")
    for name, value in inputs.items():
        if not (name == "state" or (p.fused and name in direct)):
            scratch[name] = (value.shape, value.dtype)
    scratch.update(outs)
    hbm = pl.BlockSpec(memory_space=pl.ANY)
    copies = 128
    names = (
        ["hbm_" + name for name in inputs]
        + ["hbm_" + name for name in outs]
        + list(scratch)
        + ["send_sem", "recv_sem", "back_send", "back_recv"]
        + ["load_sem", "store_sem", "state_sem"]
    )
    results = pl.pallas_call(
        functools.partial(kernel, p, names, list(inputs), list(outs)),
        out_shape=[jax.ShapeDtypeStruct(s, d) for s, d in outs.values()],
        in_specs=[hbm] * len(inputs),
        out_specs=[hbm] * len(outs),
        scratch_shapes=[pltpu.VMEM(s, d) for s, d in scratch.values()]
        + [pltpu.SemaphoreType.DMA((copies,))] * 2
        + [pltpu.SemaphoreType.DMA((p.micro, 2, p.n_z - 1))] * 2
        + [
            pltpu.SemaphoreType.DMA((len(inputs),)),
            pltpu.SemaphoreType.DMA((len(outs),)),
            pltpu.SemaphoreType.DMA((p.micro,)),
        ],
        compiler_params=pltpu.CompilerParams(
            collective_id=0, has_side_effects=True, vmem_limit_bytes=127 << 19
        ),
        name="layer",
    )(*inputs.values())
    return dict(zip(outs, results))


def hand_over(values):
    def body(*refs):
        count = len(values)
        held, sems = refs[2 * count : 3 * count], refs[3 * count :]
        taken = [
            pltpu.make_async_copy(refs[k], held[k], sems[0].at[k]) for k in range(count)
        ]
        given = [
            pltpu.make_async_copy(held[k], refs[count + k], sems[1].at[k])
            for k in range(count)
        ]
        for copy in taken:
            copy.start()
        for old, new in zip(taken, given):
            old.wait()
            new.start()
        for copy in given:
            copy.wait()

    hbm = pl.BlockSpec(memory_space=pl.ANY)
    moved = pl.pallas_call(
        body,
        out_shape=[jax.ShapeDtypeStruct(v.shape, v.dtype) for v in values.values()],
        in_specs=[hbm] * len(values),
        out_specs=[hbm] * len(values),
        scratch_shapes=[pltpu.VMEM(v.shape, v.dtype) for v in values.values()]
        + [pltpu.SemaphoreType.DMA((len(values),))] * 2,
        name="hand_over",
    )(*values.values())
    return dict(zip(values, moved))


WEIGHTS = (
    "w_query",
    "w_key",
    "w_value",
    "w_out",
    "w_up",
    "b_up",
    "w_down",
    "b_down",
    "gain_one",
    "bias_one",
    "gain_two",
    "bias_two",
    "w_halt",
)


def per_device(state, segment, parent, halting, ponder, cot_state, cot_halt, *weights):
    micro, rows, width = state.shape
    given = dict(zip(WEIGHTS, weights))
    n_dp, n_z = lax.axis_size("dp"), lax.axis_size("fsdp")
    part, hidden = given["w_query"].shape[0], given["w_up"].shape[1]
    fused = n_dp == 8 and part % 16 == 0 and part <= 128
    p = Plan(micro, rows, width, hidden, parent.shape[2], n_dp, n_z, fused)
    inputs = dict(
        state=state,
        seg=segment,
        parent=parent,
        halting=halting,
        ponder=ponder,
        cot=cot_state,
        cot_halt=cot_halt,
    )
    if fused:
        for name, value in given.items():
            inputs[name] = value if value.ndim == 2 else value.reshape(1, -1)
        out = hand_over(run_kernel(p, inputs))
        grads = []
        for name in WEIGHTS:
            value = out["g_" + name[2:]] if name.startswith("w_") and name != "w_halt" else out["g_" + name]
            grads.append(value.reshape(given[name].shape))
    else:
        axes = ("dp", "fsdp")
        full = {k: lax.all_gather(v, axes, axis=0, tiled=True) for k, v in given.items()}
        inputs["wa"] = jnp.concatenate([full[k] for k in WEIGHTS[:5]], axis=1)
        inputs["wd"] = full["w_down"]
        rows_f32 = [full[k].astype(F32) for k in WEIGHTS[7:]]
        rows_f32 += [jnp.zeros((width,), F32)] * 2
        inputs["vec"] = jnp.stack(rows_f32)
        inputs["bup"] = full["b_up"].astype(F32).reshape(1, -1)
        out = run_kernel(p, inputs)
        whole = [out["ga"][:, k * width : (k + 1) * width] for k in range(4)]
        whole += [out["ga"][:, 4 * width :], out["gbup"][0], out["gd"]]
        whole += [out["gvec"][k] for k in range(VECTORS)]
        grads = [
            lax.psum_scatter(g, axes, scatter_dimension=0, tiled=True) for g in whole
        ]
    return (out["new_state"], out["new_halting"], out["new_ponder"], out["gstate"], *grads)


def solution(mesh):
    tokens, flags = P(None, ("dp", "fsdp"), None), P(None, ("dp", "fsdp"))
    matrix, vector = P(("dp", "fsdp"), None), P(("dp", "fsdp"))
    weights = tuple(
        matrix if name in ("w_query", "w_key", "w_value", "w_out", "w_up", "w_down") else vector
        for name in WEIGHTS
    )
    return jax.shard_map(
        per_device,
        mesh=mesh,
        in_specs=(tokens, P(None, "dp"), P(None, "dp", None), flags, flags, tokens, flags)
        + weights,
        out_specs=(tokens, flags, flags, tokens) + weights,
        check_vma=False,
    )
```

time: 261 us -> 167 us (0.64)
  Pallas kernels: 247 us -> 166 us
  local copies, waits for them, and re-layouts: 13.2 us -> 0 us
    pallas_call x1 -> x2, Pallas kernels: 247 us -> 166 us  [the longest x1 163 us: run_kernel(): pl.pallas_call(functools.partial(kernel, p, names, list(inputs), list(out...]
    unnamed x50 -> x0, local copies, waits for them, and re-layouts: 13.2 us -> none
where the time goes in v2:
time: 167 us
  Pallas kernels  166 us (99%)
    pallas_call x1, Pallas kernels, run_kernel(): pl.pallas_call(functools.partial(kernel, p, names, list(inputs), list(out...  163 us

profile of v2, /device:TPU:0, one launch (start us, length us, event | category | flops | bytes accessed | tf_op | source)
XLA Modules:
  0.0 166.8 jit_solution(1299842771442280268)
XLA Ops:
  0.7 162.7 %layer.1 = (bf16[3,256,512]{2,1,0:T(8,128)(2,1)}, f32[3,256]{1,0:T(4,128)}, f32[3,256]{1,0:T(4,128)}, f32[3,256,512]{2,1,0:T(8,128)}, f32[16,512]{1,0:T(8,128)},...) custom-call(bf16[3,256,512]{2,1,0:T(8,128)(2,1)} %refs_0_.1, ...), custom_call_target="tpu_custom_call" | custom-call | tf_op jit(solution)/shard_map/layer/pallas_call | solution.py:1105
  163.4 3.3 %hand_over.1 = (bf16[3,256,512]{2,1,0:T(8,128)(2,1)}, f32[3,256]{1,0:T(4,128)}, f32[3,256]{1,0:T(4,128)}, f32[3,256,512]{2,1,0:T(8,128)}, f32[16,512]{1,0:T(8,12...) custom-call(bf16[3,256,512]{2,1,0:T(8,128)(2,1)} %get-tuple-element., ...), custom_call_target="tpu_custom_call" | custom-call | tf_op jit(solution)/shard_map/hand_over/pallas_call | solution.py:1146

commit v3 on v2

--- a/solution.py
+++ b/solution.py
@@ -37,6 +37,12 @@
 
 def iota(shape, axis):
     return lax.broadcasted_iota(jnp.int32, shape, axis)
+
+
+def split_at(values, size):
+    if size & (size - 1) == 0:
+        return values >> (size.bit_length() - 1), values & (size - 1)
+    return lax.div(values, size), lax.rem(values, size)
 
 
 def flip(index, bit):
@@ -199,7 +205,7 @@
     finish(p.pairs - 1)
 
 
-def transition(p, m, z, r, between):
+def transition(p, m, z, r, between, down_done, up_done):
     w = p.width
     rows = p.rows
     vec = lambda k: r.vec[k : k + 1, :]
@@ -291,17 +297,21 @@
     r.acc[...] = dy2
     r.gstate[m] = (1.0 - weight) * cot
 
-    @pl.loop(0, p.hidden // w)
-    def _(j):
-        at = pl.ds(pl.multiple_of(j * w, w), w)
-        at_up = pl.ds(pl.multiple_of(4 * w + j * w, w), w)
-        block = pl.ds(pl.multiple_of(j * rows, rows), rows)
+    for j in range(p.hidden // w):
+        at = slice(j * w, (j + 1) * w)
+        block = slice(j * rows, (j + 1) * rows)
+        r.gd[at, :] += tn(r.dkv[block, 0:w], r.dg[...])
+        down_done(j)
+    for j in range(p.hidden // w):
+        at = slice(j * w, (j + 1) * w)
+        at_up = slice((4 + j) * w, (5 + j) * w)
+        block = slice(j * rows, (j + 1) * rows)
         dz = nt(r.dg[...], r.wd[at, :]) * r.dkv[block, w : 2 * w].astype(F32)
         r.gbup[:, at] += col_sum(dz)
         dzb = dz.astype(BF16)
         r.acc[...] += nt(dzb, r.wa[:, at_up])
         r.ga[:, at_up] += tn(r.u[...], dzb)
-        r.gd[at, :] += tn(r.dkv[block, 0:w], r.dg[...])
+        up_done(j)
 
     dn1 = r.acc[...]
     xh1 = r.xh1[...]
@@ -314,20 +324,23 @@
     r.dot[...] = nt(r.wa[:, w_out], da)
 
 
-def attention_backward(p, r, inside):
+def attention_backward(p, m, z, r, back, inside):
     w = p.width
-
-    @pl.loop(0, p.pairs)
-    def _(i):
-        inside(i)
-        lanes = pl.ds(pl.multiple_of(i * p.pair, p.pair), p.pair)
-        low = pl.ds(pl.multiple_of(i * p.pair, p.pair), p.head)
-        high = pl.ds(pl.multiple_of(i * p.pair + p.head, p.head), p.head)
+    size = p.tree // 2
+
+    @pl.when(m >= 2)
+    def _():
+        back.left(m - 2)
+
+    def ready(i):
+        low = slice(i * p.pair, i * p.pair + p.head)
+        high = slice(i * p.pair + p.head, (i + 1) * p.pair)
         inv = r.inv[i]
+        full, q = r.dofull.at[i % 2], r.qpair.at[i % 2]
         do_a = (r.dot[low, :] * inv[0:1, 0 : p.rows]).astype(BF16)
         do_b = (r.dot[high, :] * inv[0:1, p.rows :]).astype(BF16)
-        r.dofull[0 : p.head, 0 : p.rows] = do_a
-        r.dofull[p.head : p.pair, p.rows :] = do_b
+        full[0 : p.head, 0 : p.rows] = do_a
+        full[p.head : p.pair, p.rows :] = do_b
         inner = jnp.concatenate(
             [
                 col_sum(do_a.astype(F32) * r.ot[low, :]),
@@ -337,38 +350,37 @@
         )
         rough = (-inner).astype(BF16).astype(F32)
         row = iota((16, 2 * p.rows), 0)
-        r.dofull[128:144, :] = jnp.where(
+        full[128:144, :] = jnp.where(
             row == 0, rough, jnp.where(row == 1, -inner - rough, 0.0)
         ).astype(BF16)
+        q[0 : p.head, 0 : p.rows] = r.qt[low, :]
+        q[p.head : p.pair, p.rows :] = r.qt[high, :]
+
+    ready(0)
+    for i in range(p.pairs):
+        inside(i)
+        lanes = slice(i * p.pair, (i + 1) * p.pair)
+        lanes_v = slice(w + i * p.pair, w + (i + 1) * p.pair)
         r.vfull[:, 0:128] = r.v[:, lanes]
-        fill_pair(p, r.qfull, r.qt, i)
-        lanes_v = pl.ds(pl.multiple_of(w + i * p.pair, p.pair), p.pair)
-        half = p.tree // 2
+        total = None
         for c in range(2):
-            at = slice(c * half, (c + 1) * half)
-            dp = nn(r.vfull[at, :], r.dofull[...])
+            at = slice(c * size, (c + 1) * size)
+            dp = nn(r.vfull[at, :], r.dofull[i % 2])
+            if c == 0 and i + 1 < p.pairs:
+                ready(i + 1)
             e = r.e[i, at, :]
             ds = (e.astype(F32) * dp).astype(BF16)
-            r.ds[at, :] = ds
-            r.dkv[at, lanes] = (nt(ds, r.qfull[0:128, :]) * LN2).astype(BF16)
-            r.dkv[at, lanes_v] = nt(e, r.dofull[0:128, :]).astype(BF16)
-        dq = nn(r.vt[lanes, :], r.ds[...]) * (p.head**-0.5)
-        r.dqt[low, :] = dq[0 : p.head, 0 : p.rows].astype(BF16)
-        r.dqt[high, :] = dq[p.head : p.pair, p.rows :].astype(BF16)
-
-
-def back_to_input(p, m, z, r, back):
-    w = p.width
-    r.dq[...] = r.dqt[...].T
-    r.gstate[m] += nt(r.dq[...], r.wa[:, 0:w])
-
-    @pl.when(m >= 2)
-    def _():
-        back.left(m - 2)
-
-    @pl.loop(0, p.n_z)
-    def _(b):
-        at = pl.ds(pl.multiple_of(b * p.rows, p.rows), p.rows)
+            r.ds[c] = ds
+            r.dkv[at, lanes] = (nt(ds, r.qpair[i % 2]) * LN2).astype(BF16)
+            r.dkv[at, lanes_v] = nt(e, r.dofull[i % 2, 0:128, :]).astype(BF16)
+            part = nn(r.vt[lanes, at], r.ds[c])
+            total = part if total is None else total + part
+        dq = (total * (p.head**-0.5)).astype(BF16)
+        r.dqt[i * p.pair : i * p.pair + p.head, :] = dq[0 : p.head, 0 : p.rows]
+        r.dqt[i * p.pair + p.head : (i + 1) * p.pair, :] = dq[p.head : p.pair, p.rows :]
+
+    for b in range(p.n_z):
+        at = slice(b * p.rows, (b + 1) * p.rows)
         dh = nt(r.dkv[at, :], r.wa[:, w : 3 * w])
         r.dh[lax.rem(m, 2), b] = dh.astype(BF16)
 
@@ -377,6 +389,8 @@
             r.gstate[m] += dh
 
     back.step(m, 0)
+    r.dq[...] = r.dqt[...].T
+    r.gstate[m] += nt(r.dq[...], r.wa[:, 0:w])
 
 
 def input_gradients(p, z, r):
@@ -545,15 +559,17 @@
 
 
 class Spread:
-    def __init__(self, p, piece, dp, z, flow):
+    def __init__(self, p, piece, dp, z, flow, far):
         ref, part, c0, c1 = piece
-        size = part * p.n_z
+        size = part * p.n_z // 2
+        side = lax.div(z, p.n_z // 2)
+        side = 1 - side if far else side
         mid = (c0 + c1) // 2 if c1 - c0 >= 256 else c1
         self.split = mid < c1
 
         def made(block, turn, a, b):
-            mine = ref.at[rows_of(block, size), a:b]
-            theirs = ref.at[rows_of(flip(block, turn), size), a:b]
+            mine = ref.at[rows_of(2 * block + side, size), a:b]
+            theirs = ref.at[rows_of(2 * flip(block, turn) + side, size), a:b]
             to = (flip(dp, turn), z)
             return Copy(flow, lambda: (mine, mine, to), lambda: (theirs, theirs, to))
 
@@ -594,9 +610,9 @@
 
 
 class Reduce:
-    def __init__(self, p, g, part, c0, c1, bufs, dp, z, flow):
+    def __init__(self, p, g, part, c0, c1, bufs, dp, z, flow, by_rows=False):
         self.p, self.g, self.part, self.c0, self.c1 = p, g, part, c0, c1
-        self.dp, self.z = dp, z
+        self.dp, self.z, self.by_rows = dp, z, by_rows
         self.size = size = part * p.n_z
         self.cols = cols = c1 - c0
         self.mid = mid = cols // 2 if cols >= 256 else cols
@@ -610,7 +626,17 @@
         def made(src, dst, to):
             return Copy(flow, lambda: (src, dst, to))
 
-        self.core = made(s1.at[:, 0:cols], r1.at[:, 0:cols], core)
+        if by_rows:
+            self.chunks = [
+                (slice(k * size, (k + 1) * size), slice(0, cols)) for k in range(4)
+            ]
+        else:
+            wide = min(p.width, cols)
+            self.chunks = [
+                (slice(0, 4 * size), slice(k * wide, (k + 1) * wide))
+                for k in range(cols // wide)
+            ]
+        self.core = [made(s1.at[at], r1.at[at], core) for at in self.chunks]
         self.a1 = made(s1.at[0 : 2 * size, 0:mid], r2.at[:, 0:mid], x)
         self.a2 = made(s1.at[0:size, 0:mid], r3.at[:, 0:mid], y)
         if self.split:
@@ -621,75 +647,76 @@
             peer = lax.rem(z + i, p.n_z)
             self.zs.append(made(s4.at[i - 1, :, 0:cols], r4.at[i - 1, :, 0:cols], (dp, peer)))
 
-    def _rows(self, block, a, b):
-        return self.g.at[rows_of(block, self.size), self.c0 + a : self.c0 + b]
-
-    def _put(self, slot, block, a, b):
-        size = self.size
-        self.s1[slot * size : (slot + 1) * size, a:b] = self._rows(block, a, b)[...].astype(BF16)
-
-    def _add(self, buf, slot, block, a, b):
-        size = self.size
-        self._rows(block, a, b)[...] += buf[slot * size : (slot + 1) * size, a:b].astype(F32)
-
-    def core_start(self):
-        for k, block in enumerate(self.order):
-            self._put(k, flip(block, 1), 0, self.cols)
-        self.core.start()
+    def _sum(self, block, a, b, got=(), sub=None):
+        first, count = (0, self.size) if sub is None else (sub * self.part, self.part)
+
+        def at(start):
+            return pl.ds(pl.multiple_of(start + first, self.part), count)
+
+        total = self.g[at(block * self.size), self.c0 + a : self.c0 + b]
+        for buf, slot in got:
+            total = total + buf[at(slot * self.size), a:b].astype(F32)
+        return total
+
+    def _first(self, block):
+        return self.r1, lax.div(block, 2)
+
+    def _put(self, slot, a, b, total):
+        self.s1[rows_of(slot, self.size), a:b] = total.astype(BF16)
+
+    def core_start(self, k):
+        _, lanes = self.chunks[k]
+        a, b = lanes.start, lanes.stop
+        theirs = 1 - lax.rem(self.dp, 2)
+        for slot in (k,) if self.by_rows else range(4):
+            self._put(slot, a, b, self._sum(2 * slot + theirs, a, b))
+        self.core[k].start()
 
     def core_end(self):
         order, mid, cols = self.order, self.mid, self.cols
-        self.core.arrived()
-        self.core.left()
-        for k, block in ((1, order[1]), (3, order[3])):
-            self._add(self.r1, k, block, 0, mid)
-        self._put(0, order[1], 0, mid)
-        self._put(1, order[3], 0, mid)
+        for copy in self.core:
+            copy.arrived()
+        for copy in self.core:
+            copy.left()
+        for slot, k in ((0, 1), (1, 3)):
+            self._put(slot, 0, mid, self._sum(order[k], 0, mid, [self._first(order[k])]))
         self.a1.start()
         if self.split:
-            for k, block in ((2, order[2]), (3, order[3])):
-                self._add(self.r1, k, block, mid, cols)
-            self._put(0, order[2], mid, cols)
-            self._put(1, order[3], mid, cols)
+            for slot, k in ((0, 2), (1, 3)):
+                one = self._sum(order[k], mid, cols, [self._first(order[k])])
+                self._put(slot, mid, cols, one)
             self.b1.start()
-            for k, block in ((0, order[0]), (1, order[1])):
-                self._add(self.r1, k, block, mid, cols)
-        for k, block in ((0, order[0]), (2, order[2])):
-            self._add(self.r1, k, block, 0, mid)
 
     def plane_middle(self):
         order, mid, cols = self.order, self.mid, self.cols
         self.a1.arrived()
-        self._add(self.r2, 1, order[2], 0, mid)
         self.a1.left()
-        self._put(0, order[2], 0, mid)
+        got = [self._first(order[2]), (self.r2, 1)]
+        self._put(0, 0, mid, self._sum(order[2], 0, mid, got))
         self.a2.start()
-        self._add(self.r2, 0, order[0], 0, mid)
         if self.split:
             self.b1.arrived()
-            self._add(self.r2, 1, order[1], mid, cols)
             self.b1.left()
-            self._put(0, order[1], mid, cols)
+            got = [self._first(order[1]), (self.r2, 1)]
+            self._put(0, mid, cols, self._sum(order[1], mid, cols, got))
             self.b2.start()
-            self._add(self.r2, 0, order[0], mid, cols)
+
+    def _own(self, place):
+        got = [self._first(self.dp), (self.r2, 0), (self.r3, 0)]
+        return self._sum(self.dp, 0, self.cols, got, place)
 
     def plane_end(self):
         self.a2.arrived()
         if self.split:
             self.b2.arrived()
-        self._add(self.r3, 0, self.dp, 0, self.cols)
-        p, part = self.p, self.part
-        for i in range(1, p.n_z):
-            peer = lax.rem(self.z + i, p.n_z)
-            self.s4[i - 1, :, 0 : self.cols] = self.g[
-                rows_of(self.dp * p.n_z + peer, part), self.c0 : self.c1
-            ].astype(BF16)
+        for i in range(1, self.p.n_z):
+            peer = lax.rem(self.z + i, self.p.n_z)
+            self.s4[i - 1, :, 0 : self.cols] = self._own(peer).astype(BF16)
             self.zs[i - 1].start()
 
     def total(self):
-        p = self.p
-        total = self.g[rows_of(self.dp * p.n_z + self.z, self.part), self.c0 : self.c1]
-        for i in range(1, p.n_z):
+        total = self._own(self.z)
+        for i in range(1, self.p.n_z):
             self.zs[i - 1].arrived()
             total = total + self.r4[i - 1, :, 0 : self.cols].astype(F32)
         return total
@@ -701,9 +728,9 @@
     def spread(k, part, total):
         g = r.wsf[pl.ds(k, p.devices, stride=16), :].astype(BF16)
         lane, column = iota((128, total), 0), iota((128, total), 1)
-        place = jnp.where((lane < part) & (lax.rem(column, part) == lane), 1.0, 0.0)
+        place = jnp.where(split_at(column, part)[1] == lane, 1.0, 0.0)
         full = nn(g, place.astype(BF16))
-        mine = lax.div(iota((p.devices, total), 1), part) == iota((p.devices, total), 0)
+        mine = split_at(iota((p.devices, total), 1), part)[0] == iota((p.devices, total), 0)
         return col_sum(jnp.where(mine, full, 0.0))
 
     for k in range(VECTORS):
@@ -715,14 +742,12 @@
     r.gs[...] = jnp.zeros(r.gs.shape, F32)
 
     def collect(k, row, part, total):
-        mine = lax.div(iota((p.devices, total), 1), part) == iota((p.devices, total), 0)
+        mine = split_at(iota((p.devices, total), 1), part)[0] == iota((p.devices, total), 0)
         full = jnp.where(mine, row, 0.0)
         high = full.astype(BF16)
         rest = (full - high.astype(F32)).astype(BF16)
         lane, column = iota((128, total), 0), iota((128, total), 1)
-        place = jnp.where(
-            (lane < part) & (lax.rem(column, part) == lane), 1.0, 0.0
-        ).astype(BF16)
+        place = jnp.where(split_at(column, part)[1] == lane, 1.0, 0.0).astype(BF16)
         r.gs[pl.ds(k, p.devices, stride=16), :] = nt(high, place) + nt(rest, place)
 
     for k in range(VECTORS):
@@ -768,6 +793,7 @@
     r.gbup[...] = jnp.zeros(r.gbup.shape, F32)
     r.qfull[...] = jnp.zeros(r.qfull.shape, BF16)
     r.dofull[...] = jnp.zeros(r.dofull.shape, BF16)
+    r.qpair[...] = jnp.zeros(r.qpair.shape, BF16)
     r.vo[128:144, :] = jnp.ones((16, p.tree), BF16)
     lane = iota((p.tree, 128), 1)
     r.vfull[:, 128:256] = jnp.where(lane < 2, 1.0, 0.0).astype(BF16)
@@ -822,10 +848,12 @@
                 return ref.at[rows_of(dp * p.n_z + b, part), c0:c1]
 
             rods.append(Line(p, block, dp, z, flow))
-        spreads = [Spread(p, piece, dp, z, flow) for piece in parts]
+        spreads, fars = (
+            [Spread(p, piece, dp, z, flow, far) for piece in parts] for far in (False, True)
+        )
         sums = [
             Reduce(p, r.ga, p.part, 3 * w, p.cols, buffers(r, "f"), dp, z, flow),
-            Reduce(p, r.gd, p.part_h, 0, w, [r.k] + buffers(r, "d"), dp, z, flow),
+            Reduce(p, r.gd, p.part_h, 0, w, buffers(r, "d"), dp, z, flow, by_rows=True),
             Reduce(p, r.gs, 16, 0, 128, buffers(r, "e"), dp, z, flow),
             Reduce(p, r.ga, p.part, 0, 3 * w, [r.q0] + buffers(r, "b"), dp, z, flow),
         ]
@@ -839,23 +867,30 @@
         for rod in rods:
             rod.step(0)
         make_signal(p, r)
-        for k in range(1, steps):
-            for rod in rods:
-                rod.step(k)
-            lines[0].step(k - 1)
-            if k == 1:
-                clear(p, r)
         for rod, spread in zip(rods, spreads):
-            rod.step(steps)
+            rod.step(1)
             spread.start()
-        lines[0].step(steps - 1)
+        clear(p, r)
+        for rod in rods:
+            rod.step(2)
+        lines[0].step(0)
+        for rod, spread, far in zip(rods, spreads, fars):
+            rod.step(3)
+            spread.middle()
+            far.start()
+        lines[0].step(1)
         for spread in spreads:
-            spread.middle()
-        spreads[0].late()
-        spreads[0].end()
-        lines[0].step(steps)
+            spread.late()
+        fars[0].middle()
+        lines[0].step(2)
         if p.micro > 1:
             lines[1].step(0)
+        fars[0].late()
+        for far in fars[1:]:
+            far.middle()
+        spreads[0].end()
+        fars[0].end()
+        lines[0].step(3)
     else:
         for k in range(steps + 1):
             for line in lines:
@@ -877,45 +912,55 @@
 
             @pl.when(m == 0)
             def _():
-                for spread in spreads[1:]:
-                    spread.late()
+                for far in fars[1:]:
+                    far.late()
 
         attention_forward(p, r)
 
-        @pl.when(m > 0)
+        @pl.when(m > 1)
         def _():
-            for k in range(1, steps - 1):
-                back.step(m - 1, k)
+            back.step(m - 2, steps)
 
         if p.fused:
 
             @pl.when(m == 1)
             def _():
                 for line in lines[2:]:
-                    line.step(steps - 1)
+                    for k in range(1, steps - 1):
+                        line.step(k)
 
             @pl.when(m == 0)
             def _():
                 if p.micro > 1:
                     for k in range(1, steps - 1):
                         lines[1].step(k)
-                for spread in spreads[1:]:
+                for spread in spreads[1:] + fars[1:]:
                     spread.end()
                 spread_vectors(p, r)
 
         def between():
+            @pl.when(m > 0)
+            def _():
+                for k in range(1, steps - 1):
+                    back.step(m - 1, k)
+
+        def down_done(j):
             if p.fused:
 
-                @pl.when(m == 0)
+                @pl.when(m == p.micro - 1)
                 def _():
-                    for line in lines[2:]:
-                        line.step(0)
-
-        transition(p, m, z, r, between)
-
-        @pl.when(m > 0)
-        def _():
-            back.step(m - 1, steps - 1)
+                    sums[1].core_start(j)
+
+        def up_done(j):
+            if p.fused:
+
+                @pl.when(m == p.micro - 1)
+                def _():
+                    sums[0].core_start(1 + j)
+                    if j == p.hidden // w - 1:
+                        sums[1].core_end()
+
+        transition(p, m, z, r, between, down_done, up_done)
 
         out = pltpu.make_async_copy(
             r.new_state.at[m], r.hbm_new_state.at[m], r.state_sem.at[m]
@@ -926,59 +971,67 @@
             @pl.when(m == 0)
             def _():
                 lines[1].step(steps - 1)
+                for line in lines[2:]:
+                    line.step(0)
+
+            @pl.when(m == 1)
+            def _():
+                for line in lines[2:]:
+                    line.step(steps - 1)
 
         r.vt[...] = r.k[...].T
         if p.fused:
 
             @pl.when(m == p.micro - 1)
             def _():
-                sums[0].core_start()
-                sums[1].core_start()
+                sums[0].core_start(0)
                 collect_vectors(p, r)
-                sums[2].core_start()
+                sums[2].core_start(0)
 
         def inside(i):
-            if p.fused:
-
-                @pl.when((m == p.micro - 1) & (i == p.pairs // 2))
+            if i == p.pairs // 2:
+
+                @pl.when(m > 0)
                 def _():
-                    for one in sums[:3]:
-                        one.core_end()
-
-        attention_backward(p, r, inside)
-        if p.fused:
-
-            @pl.when(m == 0)
-            def _():
-                for line in lines[2:]:
-                    for k in range(1, steps - 1):
-                        line.step(k)
-
-
-        @pl.when(m > 0)
-        def _():
-            back.step(m - 1, steps)
-
-        back_to_input(p, m, z, r, back)
+                    back.step(m - 1, steps - 1)
+
+            if p.fused and i == 1:
+
+                @pl.when(m == p.micro - 1)
+                def _():
+                    sums[0].core_end()
+
+            if p.fused and i == p.pairs - 1:
+
+                @pl.when(m == p.micro - 1)
+                def _():
+                    sums[2].core_end()
+
+        attention_backward(p, m, z, r, back, inside)
         input_gradients(p, z, r)
 
     if p.fused:
-        sums[3].core_start()
-        for one in sums[:3]:
-            one.plane_middle()
+        last = p.micro - 1
+        for k in range(3):
+            sums[3].core_start(k)
+        sums[1].plane_middle()
+        if last > 0:
+            back.step(last - 1, steps)
         sums[3].core_end()
-        back.step(p.micro - 1, 1)
-        for one in sums[:3]:
-            one.plane_end()
-        back.step(p.micro - 1, 2)
+        sums[2].plane_middle()
+        sums[0].plane_middle()
+        back.step(last, 1)
+        sums[1].plane_end()
+        sums[2].plane_end()
         sums[3].plane_middle()
+        back.step(last, 2)
+        sums[0].plane_end()
         sums[3].plane_end()
-        for k in range(3, steps + 1):
-            back.step(p.micro - 1, k)
+        back.step(last, 3)
+        r.g_down[...] = sums[1].total()
         total = sums[0].total()
         r.g_out[...] = total[:, 0:w]
         r.g_up[...] = total[:, w:]
-        r.g_down[...] = sums[1].total()
         r.small[...] = sums[2].total()
         for k, name in enumerate(SMALL):
             getattr(r, "g_" + name)[...] = r.small[k : k + 1, 0 : p.part]
@@ -988,6 +1041,8 @@
         r.g_key[...] = total[:, w : 2 * w]
         r.g_value[...] = total[:, 2 * w : 3 * w]
     else:
+        if p.micro > 1:
+            back.step(p.micro - 2, steps)
         for k in range(1, steps + 1):
             back.step(p.micro - 1, k)
     for m in range(max(p.micro - 2, 0), p.micro):
@@ -1001,6 +1056,18 @@
     for copy in stores.values():
         copy.wait()
     flow.finish()
+    if flow.used != copy_count(p):
+        raise ValueError("copies: %d" % flow.used)
+
+
+def copy_count(p):
+    line = 2 * (p.n_z - 1)
+    if not p.fused:
+        return p.micro * line
+    spreads = 2 * (3 * 10 + 7)
+    exchanges = 3 * (4 + p.n_z - 1) + 2 + p.n_z - 1
+    chunks = (p.cols // p.width - 3) + 4 + 1 + 3
+    return (p.micro + 4) * line + spreads + exchanges + chunks
 
 
 def run_kernel(p, inputs):
@@ -1045,7 +1112,7 @@
             shapes = [(k * size, cols) for k in (4, 4, 2, 1)]
             shapes += [(p.n_z - 1, part, cols)] * 2
             for k, shape in enumerate(shapes):
-                if k or tag in "fe":
+                if k or tag in "fed":
                     scratch[tag + str(k)] = (shape, BF16)
         scratch["q0"] = ((4 * p.part * p.n_z, 3 * w), BF16)
     else:
@@ -1067,7 +1134,7 @@
         kfull=((t, 256), BF16),
         qfull=((256, 2 * rows), BF16),
         vfull=((t, 256), BF16),
-        dofull=((256, 2 * rows), BF16),
+        dofull=((2, 256, 2 * rows), BF16),
         vo=((144, t), BF16),
         e=((p.pairs, t, 2 * rows), BF16),
         s=((t, 2 * rows), F32),
@@ -1081,9 +1148,10 @@
         u=((rows, w), BF16),
         acc=((rows, w), F32),
         dg=((rows, w), BF16),
-        ds=((t, 2 * rows), BF16),
+        ds=((2, t // 2, 2 * rows), BF16),
         dkv=((max(t, rows * (p.hidden // w)), 2 * w), BF16),
         dqt=((w, rows), BF16),
+        qpair=((2, 128, 2 * rows), BF16),
         dq=((rows, w), BF16),
         dh=((2, p.n_z, rows, w), BF16),
         dh_in=((p.micro, p.n_z + 1, rows, w), BF16),
@@ -1094,7 +1162,7 @@
             scratch[name] = (value.shape, value.dtype)
     scratch.update(outs)
     hbm = pl.BlockSpec(memory_space=pl.ANY)
-    copies = 128
+    copies = copy_count(p)
     names = (
         ["hbm_" + name for name in inputs]
         + ["hbm_" + name for name in outs]
@@ -1177,7 +1245,7 @@
     given = dict(zip(WEIGHTS, weights))
     n_dp, n_z = lax.axis_size("dp"), lax.axis_size("fsdp")
     part, hidden = given["w_query"].shape[0], given["w_up"].shape[1]
-    fused = n_dp == 8 and part % 16 == 0 and part <= 128
+    fused = n_dp == 8 and n_z == 4 and part % 16 == 0 and part <= 128
     p = Plan(micro, rows, width, hidden, parent.shape[2], n_dp, n_z, fused)
     inputs = dict(
         state=state,

time: 167 us -> 152 us (0.910)
  Pallas kernels: 166 us -> 151 us
    pallas_call x1, Pallas kernels: 163 us -> 148 us  [run_kernel(): pl.pallas_call(functools.partial(kernel, p, names, list(inputs), list(out...]
where the time goes in v3:
time: 152 us
  Pallas kernels  151 us (99%)
    pallas_call x1, Pallas kernels, run_kernel(): pl.pallas_call(functools.partial(kernel, p, names, list(inputs), list(out...  148 us
    pallas_call x1, Pallas kernels, hand_over(): pl.pallas_call(body, out_shape=[jax.ShapeDtypeStruct(v.shape, v.dtype) fo...  3.27 us

profile of v3, /device:TPU:0, one launch (start us, length us, event | category | flops | bytes accessed | tf_op | source)
XLA Modules:
  0.0 151.9 jit_solution(4315113351493811164)
XLA Ops:
  0.7 147.8 %layer.1 = (bf16[3,256,512]{2,1,0:T(8,128)(2,1)}, f32[3,256]{1,0:T(4,128)}, f32[3,256]{1,0:T(4,128)}, f32[3,256,512]{2,1,0:T(8,128)}, f32[16,512]{1,0:T(8,128)},...) custom-call(bf16[3,256,512]{2,1,0:T(8,128)(2,1)} %refs_0_.1, ...), custom_call_target="tpu_custom_call" | custom-call | tf_op jit(solution)/shard_map/layer/pallas_call | solution.py:1173
  148.4 3.3 %hand_over.1 = (bf16[3,256,512]{2,1,0:T(8,128)(2,1)}, f32[3,256]{1,0:T(4,128)}, f32[3,256]{1,0:T(4,128)}, f32[3,256,512]{2,1,0:T(8,128)}, f32[16,512]{1,0:T(8,12...) custom-call(bf16[3,256,512]{2,1,0:T(8,128)(2,1)} %get-tuple-element., ...), custom_call_target="tpu_custom_call" | custom-call | tf_op jit(solution)/shard_map/hand_over/pallas_call | solution.py:1214

commit v4 on v3

--- a/solution.py
+++ b/solution.py
@@ -336,7 +336,7 @@
         low = slice(i * p.pair, i * p.pair + p.head)
         high = slice(i * p.pair + p.head, (i + 1) * p.pair)
         inv = r.inv[i]
-        full, q = r.dofull.at[i % 2], r.qpair.at[i % 2]
+        full, q = r.dofull.at[i], r.qpair.at[i]
         do_a = (r.dot[low, :] * inv[0:1, 0 : p.rows]).astype(BF16)
         do_b = (r.dot[high, :] * inv[0:1, p.rows :]).astype(BF16)
         full[0 : p.head, 0 : p.rows] = do_a
@@ -356,39 +356,49 @@
         q[0 : p.head, 0 : p.rows] = r.qt[low, :]
         q[p.head : p.pair, p.rows :] = r.qt[high, :]
 
+    side = lax.div(z, p.n_z // 2)
     ready(0)
-    for i in range(p.pairs):
-        inside(i)
-        lanes = slice(i * p.pair, (i + 1) * p.pair)
-        lanes_v = slice(w + i * p.pair, w + (i + 1) * p.pair)
-        r.vfull[:, 0:128] = r.v[:, lanes]
-        total = None
-        for c in range(2):
-            at = slice(c * size, (c + 1) * size)
-            dp = nn(r.vfull[at, :], r.dofull[i % 2])
+    for c in range(2):
+        half = side if c else 1 - side
+        at = pl.ds(pl.multiple_of(half * size, size), size)
+        for i in range(p.pairs):
+            inside(c * p.pairs + i)
+            lanes = slice(i * p.pair, (i + 1) * p.pair)
+            lanes_v = slice(w + i * p.pair, w + (i + 1) * p.pair)
+            r.vfull[at, 0:128] = r.v[at, lanes]
+            dp = nn(r.vfull[at, :], r.dofull[i])
             if c == 0 and i + 1 < p.pairs:
                 ready(i + 1)
             e = r.e[i, at, :]
             ds = (e.astype(F32) * dp).astype(BF16)
-            r.ds[c] = ds
-            r.dkv[at, lanes] = (nt(ds, r.qpair[i % 2]) * LN2).astype(BF16)
-            r.dkv[at, lanes_v] = nt(e, r.dofull[i % 2, 0:128, :]).astype(BF16)
-            part = nn(r.vt[lanes, at], r.ds[c])
-            total = part if total is None else total + part
-        dq = (total * (p.head**-0.5)).astype(BF16)
-        r.dqt[i * p.pair : i * p.pair + p.head, :] = dq[0 : p.head, 0 : p.rows]
-        r.dqt[i * p.pair + p.head : (i + 1) * p.pair, :] = dq[p.head : p.pair, p.rows :]
-
-    for b in range(p.n_z):
-        at = slice(b * p.rows, (b + 1) * p.rows)
-        dh = nt(r.dkv[at, :], r.wa[:, w : 3 * w])
-        r.dh[lax.rem(m, 2), b] = dh.astype(BF16)
-
-        @pl.when(z == b)
-        def _():
-            r.gstate[m] += dh
-
-    back.step(m, 0)
+            r.ds[...] = ds
+            r.dkv[at, lanes] = (nt(ds, r.qpair[i]) * LN2).astype(BF16)
+            r.dkv[at, lanes_v] = nt(e, r.dofull[i, 0:128, :]).astype(BF16)
+            dq = nn(r.vt[lanes, at], r.ds[...]) * (p.head**-0.5)
+            low = slice(i * p.pair, i * p.pair + p.head)
+            high = slice(i * p.pair + p.head, (i + 1) * p.pair)
+            if c == 0:
+                r.dqt[low, :] = dq[0 : p.head, 0 : p.rows].astype(BF16)
+                r.dqt[high, :] = dq[p.head : p.pair, p.rows :].astype(BF16)
+            else:
+                one = r.dqt[low, :].astype(F32) + dq[0 : p.head, 0 : p.rows]
+                two = r.dqt[high, :].astype(F32) + dq[p.head : p.pair, p.rows :]
+                r.dqt[low, :] = one.astype(BF16)
+                r.dqt[high, :] = two.astype(BF16)
+        for k in range(p.n_z // 2):
+            b = half * (p.n_z // 2) + k
+            mine = pl.ds(pl.multiple_of(b * p.rows, p.rows), p.rows)
+            dh = nt(r.dkv[mine, :], r.wa[:, w : 3 * w])
+            r.dh[lax.rem(m, 2), b] = dh.astype(BF16)
+            if c:
+
+                @pl.when(z == b)
+                def _():
+                    r.gstate[m] += dh
+
+        if c == 0:
+            back.step(m, 0)
+
     r.dq[...] = r.dqt[...].T
     r.gstate[m] += nt(r.dq[...], r.wa[:, 0:w])
 
@@ -723,10 +733,10 @@
 
 
 def spread_vectors(p, r):
-    r.wsf[...] = r.ws[...].astype(F32)
+    r.gs[...] = r.ws[...].astype(F32)
 
     def spread(k, part, total):
-        g = r.wsf[pl.ds(k, p.devices, stride=16), :].astype(BF16)
+        g = r.gs[pl.ds(k, p.devices, stride=16), :].astype(BF16)
         lane, column = iota((128, total), 0), iota((128, total), 1)
         place = jnp.where(split_at(column, part)[1] == lane, 1.0, 0.0)
         full = nn(g, place.astype(BF16))
@@ -989,19 +999,19 @@
                 sums[2].core_start(0)
 
         def inside(i):
-            if i == p.pairs // 2:
+            if i == p.pairs + 1:
 
                 @pl.when(m > 0)
                 def _():
                     back.step(m - 1, steps - 1)
 
-            if p.fused and i == 1:
+            if p.fused and i == 2:
 
                 @pl.when(m == p.micro - 1)
                 def _():
                     sums[0].core_end()
 
-            if p.fused and i == p.pairs - 1:
+            if p.fused and i == p.pairs + 2:
 
                 @pl.when(m == p.micro - 1)
                 def _():
@@ -1014,20 +1024,19 @@
         last = p.micro - 1
         for k in range(3):
             sums[3].core_start(k)
+        back.step(last, 1)
         sums[1].plane_middle()
-        if last > 0:
-            back.step(last - 1, steps)
         sums[3].core_end()
         sums[2].plane_middle()
         sums[0].plane_middle()
-        back.step(last, 1)
         sums[1].plane_end()
+        back.step(last, 2)
+        sums[3].plane_middle()
         sums[2].plane_end()
-        sums[3].plane_middle()
-        back.step(last, 2)
         sums[0].plane_end()
         sums[3].plane_end()
         back.step(last, 3)
+        back.step(last - 1, steps)
         r.g_down[...] = sums[1].total()
         total = sums[0].total()
         r.g_out[...] = total[:, 0:w]
@@ -1091,7 +1100,6 @@
             wa=((w, p.cols), BF16),
             wd=((p.hidden, w), BF16),
             ws=((p.devices * 16, 128), BF16),
-            wsf=((p.devices * 16, 128), F32),
             small=((16, 128), F32),
             vec=((8, w), F32),
             bup=((1, p.hidden), F32),
@@ -1134,7 +1142,7 @@
         kfull=((t, 256), BF16),
         qfull=((256, 2 * rows), BF16),
         vfull=((t, 256), BF16),
-        dofull=((2, 256, 2 * rows), BF16),
+        dofull=((p.pairs, 256, 2 * rows), BF16),
         vo=((144, t), BF16),
         e=((p.pairs, t, 2 * rows), BF16),
         s=((t, 2 * rows), F32),
@@ -1148,10 +1156,10 @@
         u=((rows, w), BF16),
         acc=((rows, w), F32),
         dg=((rows, w), BF16),
-        ds=((2, t // 2, 2 * rows), BF16),
+        ds=((t // 2, 2 * rows), BF16),
         dkv=((max(t, rows * (p.hidden // w)), 2 * w), BF16),
         dqt=((w, rows), BF16),
-        qpair=((2, 128, 2 * rows), BF16),
+        qpair=((p.pairs, 128, 2 * rows), BF16),
         dq=((rows, w), BF16),
         dh=((2, p.n_z, rows, w), BF16),
         dh_in=((p.micro, p.n_z + 1, rows, w), BF16),

time: 152 us -> 149 us (0.980)
  Pallas kernels: 151 us -> 148 us
    pallas_call x1, Pallas kernels: 148 us -> 145 us  [run_kernel(): pl.pallas_call(functools.partial(kernel, p, names, list(inputs), list(out...]
where the time goes in v4:
time: 149 us
  Pallas kernels  148 us (99%)
    pallas_call x1, Pallas kernels, run_kernel(): pl.pallas_call(functools.partial(kernel, p, names, list(inputs), list(out...  145 us
    pallas_call x1, Pallas kernels, hand_over(): pl.pallas_call(body, out_shape=[jax.ShapeDtypeStruct(v.shape, v.dtype) fo...  3.27 us

profile of v4, /device:TPU:0, one launch (start us, length us, event | category | flops | bytes accessed | tf_op | source)
XLA Modules:
  0.0 149.1 jit_solution(12027752767389366329)
XLA Ops:
  0.7 145.0 %layer.1 = (bf16[3,256,512]{2,1,0:T(8,128)(2,1)}, f32[3,256]{1,0:T(4,128)}, f32[3,256]{1,0:T(4,128)}, f32[3,256,512]{2,1,0:T(8,128)}, f32[16,512]{1,0:T(8,128)},...) custom-call(bf16[3,256,512]{2,1,0:T(8,128)(2,1)} %refs_0_.1, ...), custom_call_target="tpu_custom_call" | custom-call | tf_op jit(solution)/shard_map/layer/pallas_call | solution.py:1181
  145.6 3.3 %hand_over.1 = (bf16[3,256,512]{2,1,0:T(8,128)(2,1)}, f32[3,256]{1,0:T(4,128)}, f32[3,256]{1,0:T(4,128)}, f32[3,256,512]{2,1,0:T(8,128)}, f32[16,512]{1,0:T(8,12...) custom-call(bf16[3,256,512]{2,1,0:T(8,128)(2,1)} %get-tuple-element., ...), custom_call_target="tpu_custom_call" | custom-call | tf_op jit(solution)/shard_map/hand_over/pallas_call | solution.py:1222

commit v5 on v4

--- a/solution.py
+++ b/solution.py
@@ -1030,8 +1030,8 @@
         sums[2].plane_middle()
         sums[0].plane_middle()
         sums[1].plane_end()
+        sums[3].plane_middle()
         back.step(last, 2)
-        sums[3].plane_middle()
         sums[2].plane_end()
         sums[0].plane_end()
         sums[3].plane_end()

time: 149 us -> 149 us (level)
  no operation moved by 1% of the time
where the time goes in v5:
time: 149 us
  Pallas kernels  148 us (99%)
    pallas_call x1, Pallas kernels, run_kernel(): pl.pallas_call(functools.partial(kernel, p, names, list(inputs), list(out...  145 us
    pallas_call x1, Pallas kernels, hand_over(): pl.pallas_call(body, out_shape=[jax.ShapeDtypeStruct(v.shape, v.dtype) fo...  3.27 us

profile of v5, /device:TPU:0, one launch (start us, length us, event | category | flops | bytes accessed | tf_op | source)
XLA Modules:
  0.0 149.1 jit_solution(3009136639225508149)
XLA Ops:
  0.7 145.0 %layer.1 = (bf16[3,256,512]{2,1,0:T(8,128)(2,1)}, f32[3,256]{1,0:T(4,128)}, f32[3,256]{1,0:T(4,128)}, f32[3,256,512]{2,1,0:T(8,128)}, f32[16,512]{1,0:T(8,128)},...) custom-call(bf16[3,256,512]{2,1,0:T(8,128)(2,1)} %refs_0_.1, ...), custom_call_target="tpu_custom_call" | custom-call | tf_op jit(solution)/shard_map/layer/pallas_call | solution.py:1181
  145.6 3.3 %hand_over.1 = (bf16[3,256,512]{2,1,0:T(8,128)(2,1)}, f32[3,256]{1,0:T(4,128)}, f32[3,256]{1,0:T(4,128)}, f32[3,256,512]{2,1,0:T(8,128)}, f32[16,512]{1,0:T(8,12...) custom-call(bf16[3,256,512]{2,1,0:T(8,128)(2,1)} %get-tuple-element., ...), custom_call_target="tpu_custom_call" | custom-call | tf_op jit(solution)/shard_map/hand_over/pallas_call | solution.py:1222
